TPU v7x, 32 devices: a whole 2x2x4 slice. The times are simulated.
32 devices in a mesh: row: 8 (over z, x), col: 4 (over y, core).
Axes of the slice: x: 2, y: 2, z: 4, core: 2. Of those that a mesh axis runs over, the one named last changes fastest.
Arguments:
- layer_input: bfloat16 [16384, 768], P(('row', 'col')), may hold values from -6 to 6
- attn_gain: float32 [768], replicated, may hold values from 0.5 to 1.5
- attn_shift: float32 [768], replicated, may hold values from -2 to 2
- qkv_weight: bfloat16 [768, 3, 768], P('row', None, 'col'), may hold values from -0.21875 to 0.21875
- qkv_bias: float32 [2, 768], P(None, 'col'), may hold values from -2 to 2
- output_weight: bfloat16 [768, 768], P('row', 'col'), may hold values from -4 to 4
- output_bias: float32 [768], replicated, may hold values from -2 to 2
- mlp_gain: float32 [768], replicated, may hold values from 0.5 to 1.5
- mlp_shift: float32 [768], replicated, may hold values from -2 to 2
- up_weight: bfloat16 [768, 3072], P('row', 'col'), may hold values from -0.21875 to 0.21875
- up_bias: float32 [3072], P('col'), may hold values from -3 to 3
- down_weight: bfloat16 [768, 3072], P('row', 'col'), may hold values from -0.109375 to 0.109375
- down_bias: float32 [768], replicated, may hold values from -2 to 2
- cotangent: bfloat16 [16384, 768], P(('row', 'col')), may hold values from -6 to 6
Outputs:
- layer_output: bfloat16 [16384, 768], P(('row', 'col'))
- input_grad: float32 [16384, 768], P(('row', 'col'))
- attn_gain_grad: float32 [768], replicated
- attn_shift_grad: float32 [768], replicated
- qkv_weight_grad: float32 [768, 3, 768], P('row', None, 'col')
- qkv_bias_grad: float32 [2, 768], P(None, 'col')
- output_weight_grad: float32 [768, 768], P('row', 'col')
- output_bias_grad: float32 [768], replicated
- mlp_gain_grad: float32 [768], replicated
- mlp_shift_grad: float32 [768], replicated
- up_weight_grad: float32 [768, 3072], P('row', 'col')
- up_bias_grad: float32 [3072], P('col')
- down_weight_grad: float32 [768, 3072], P('row', 'col')
- down_bias_grad: float32 [768], replicated
- rms_values: float32 [3], replicated
All inputs are finite; a program needn't handle non-finite values.
Results may differ from a plain program's by a relative error of at most 0.013.
Values may be sent and summed in bfloat16 or wider, within the bound.
No kernel may reach another device: no remote copies, remote signals or barrier semaphores. Data moves between devices by JAX's collectives and lax.ppermute only.
A program may use at most 128 MiB of HBM per device.

v0:
```python
from functools import partial
import math

import jax
import jax.numpy as jnp
from jax import lax
from jax.sharding import PartitionSpec as P

HEAD_DIM = 64
SEQ_LEN = 1024


EPSILON = 1e-06


def split_up(array, dim, size):
    dims = array.shape
    parts = array.reshape(*dims[:dim], size, dims[dim] // size, *dims[dim + 1 :])
    return jnp.moveaxis(parts, dim, 0)


def summed_on_arrival(array, axis, dim):
    size = lax.axis_size(axis)
    parts = lax.all_to_all(split_up(array, dim, size), axis, 0, 0, tiled=True)
    return jnp.sum(parts.astype(jnp.float32), axis=0)


def in_one_piece(arrays, axis, dim, along):
    widths = [math.prod(a.shape[along:]) for a in arrays]
    both = jnp.concatenate(
        [a.reshape(*a.shape[:along], w) for a, w in zip(arrays, widths)], axis=along
    )
    out = summed_on_arrival(both, axis, dim)
    parts = jnp.split(out, [sum(widths[:k]) for k in range(1, len(widths))], axis=along)
    return tuple((b.reshape(*out.shape[:along], *a.shape[along:]) for a, b in zip(arrays, parts)))


def contract_last(left, right):
    return lax.dot_general(
        left, right, (((1,), (1,)), ((), ())), preferred_element_type=jnp.float32
    )


def contract_first(left, right):
    return lax.dot_general(
        left, right, (((0,), (0,)), ((), ())), preferred_element_type=jnp.float32
    )


def gelu_tanh(values):
    return jax.nn.gelu(values, approximate=True)


def layer_stats(resid, gain, shift):
    row_mean = jnp.mean(resid, axis=1, keepdims=True)
    variance = jnp.mean(jnp.square(resid - row_mean), axis=1, keepdims=True)
    inverse = lax.rsqrt(variance + EPSILON)
    centered = (resid - row_mean) * inverse
    normed = (centered * gain + shift).astype(jnp.bfloat16)
    gathered = lax.all_gather(normed, "col", axis=0, tiled=True)
    return (gathered, centered, inverse)


def norm_back(grad_norm, centered, inverse, gain):
    gain_grad = jnp.sum(grad_norm * centered, axis=0)
    shift_grad = jnp.sum(grad_norm, axis=0)
    grad_hat = grad_norm * gain
    first_mean = jnp.mean(grad_hat, axis=1, keepdims=True)
    second_mean = jnp.mean(grad_hat * centered, axis=1, keepdims=True)
    grad_resid = inverse * (grad_hat - first_mean - centered * second_mean)
    return (grad_resid, gain_grad, shift_grad)


def branch_total(partial_rows):
    return lax.psum_scatter(partial_rows, "col", scatter_dimension=0, tiled=True)


def spread_grad(grad_rows):
    return lax.all_gather(grad_rows, "col", axis=0, tiled=True)


def collect_grad(partial_rows):
    return lax.psum_scatter(
        partial_rows.astype(jnp.bfloat16), "col", scatter_dimension=0, tiled=True
    ).astype(jnp.float32)


def attend_forward(seq_block, score_scale):
    query_rows = seq_block[:, 0]
    key_rows = seq_block[:, 1]
    value_rows = seq_block[:, 2]
    scores = (
        jnp.einsum("qhd,khd->hqk", query_rows, key_rows, preferred_element_type=jnp.float32)
        * score_scale
    )
    row_max = jnp.max(scores, axis=-1, keepdims=True)
    log_total = row_max + jnp.log(jnp.sum(jnp.exp(scores - row_max), axis=-1, keepdims=True))
    probabilities = jnp.exp(scores - log_total)
    attn_mixed = jnp.einsum(
        "hqk,khd->qhd",
        probabilities.astype(jnp.bfloat16),
        value_rows,
        preferred_element_type=jnp.float32,
    )
    return (attn_mixed.reshape(seq_block.shape[0], -1).astype(jnp.bfloat16), log_total[..., 0])


def attend_backward(inputs, score_scale):
    seq_block, grad_rows, log_total = inputs
    query_rows = seq_block[:, 0]
    key_rows = seq_block[:, 1]
    value_rows = seq_block[:, 2]
    scores = (
        jnp.einsum("qhd,khd->hqk", query_rows, key_rows, preferred_element_type=jnp.float32)
        * score_scale
    )
    probabilities = jnp.exp(scores - log_total[..., None])
    grad_probs = jnp.einsum(
        "qhd,khd->hqk", grad_rows, value_rows, preferred_element_type=jnp.float32
    )
    row_dots = jnp.sum(probabilities * grad_probs, axis=-1, keepdims=True)
    grad_scores = (probabilities * (grad_probs - row_dots)).astype(jnp.bfloat16)
    grad_query = (
        jnp.einsum("hqk,khd->qhd", grad_scores, key_rows, preferred_element_type=jnp.float32)
        * score_scale
    )
    grad_key = (
        jnp.einsum("hqk,qhd->khd", grad_scores, query_rows, preferred_element_type=jnp.float32)
        * score_scale
    )
    grad_value = jnp.einsum(
        "hqk,qhd->khd",
        probabilities.astype(jnp.bfloat16),
        grad_rows,
        preferred_element_type=jnp.float32,
    )
    return jnp.stack([grad_query, grad_key, grad_value], axis=1).astype(jnp.bfloat16)


def local(
    layer_input,
    attn_gain,
    attn_shift,
    qkv_weight,
    qkv_bias,
    output_weight,
    output_bias,
    mlp_gain,
    mlp_shift,
    up_weight,
    up_bias,
    down_weight,
    down_bias,
    cotangent,
):
    local_tokens = layer_input.shape[0]
    width = layer_input.shape[1]
    local_width = qkv_weight.shape[2]
    local_heads = local_width // HEAD_DIM
    group_tokens = local_tokens * lax.axis_size("col")
    seq_count = group_tokens // SEQ_LEN
    score_scale = HEAD_DIM ** (-0.5)
    qkv_full, output_full = (
        lax.all_gather(qkv_weight, "row", axis=0, tiled=True),
        lax.all_gather(output_weight, "row", axis=0, tiled=True),
    )
    up_full, down_full = (
        lax.all_gather(up_weight, "row", axis=0, tiled=True),
        lax.all_gather(down_weight, "row", axis=0, tiled=True),
    )
    residual = layer_input.astype(jnp.float32)
    attn_in, attn_hat, attn_inverse = layer_stats(residual, attn_gain, attn_shift)
    bias_rows = jnp.stack([qkv_bias[0], jnp.zeros_like(qkv_bias[0]), qkv_bias[1]])
    projected = (
        jnp.einsum("td,dcf->tcf", attn_in, qkv_full, preferred_element_type=jnp.float32) + bias_rows
    ).astype(jnp.bfloat16)
    seq_blocks = projected.reshape(seq_count, SEQ_LEN, 3, local_heads, HEAD_DIM)
    attn_mixed, log_totals = lax.map(partial(attend_forward, score_scale=score_scale), seq_blocks)
    attn_mixed = attn_mixed.reshape(group_tokens, local_width)
    attn_branch = branch_total(contract_last(attn_mixed, output_full)) + output_bias
    hidden_resid = residual + attn_branch
    mlp_in, mlp_hat, mlp_inverse = layer_stats(hidden_resid, mlp_gain, mlp_shift)
    pre_act = jnp.dot(mlp_in, up_full, preferred_element_type=jnp.float32) + up_bias
    activated = gelu_tanh(pre_act).astype(jnp.bfloat16)
    mlp_branch = branch_total(contract_last(activated, down_full)) + down_bias
    result = hidden_resid + mlp_branch
    grad_out = cotangent.astype(jnp.float32)
    down_bias_grad = jnp.sum(grad_out, axis=0)
    grad_mlp = spread_grad(cotangent)
    down_grad = contract_first(grad_mlp, activated)
    grad_act = jnp.dot(grad_mlp, down_full, preferred_element_type=jnp.float32)
    grad_pre = jax.vjp(gelu_tanh, pre_act)[1](grad_act)[0].astype(jnp.bfloat16)
    up_grad = contract_first(mlp_in, grad_pre)
    up_bias_grad = jnp.sum(grad_pre.astype(jnp.float32), axis=0)
    grad_mlp_in = collect_grad(contract_last(grad_pre, up_full))
    mlp_resid_grad, mlp_gain_grad, mlp_shift_grad = norm_back(
        grad_mlp_in, mlp_hat, mlp_inverse, mlp_gain
    )
    up_sum, down_sum = (
        lax.psum_scatter(up_grad, "row", scatter_dimension=0, tiled=True),
        lax.psum_scatter(down_grad, "row", scatter_dimension=0, tiled=True),
    )
    hidden_grad = grad_out + mlp_resid_grad
    grad_attn_low = hidden_grad.astype(jnp.bfloat16)
    output_bias_grad = jnp.sum(grad_attn_low.astype(jnp.float32), axis=0)
    grad_attn = spread_grad(grad_attn_low)
    output_grad = contract_first(grad_attn, attn_mixed)
    grad_mixed = jnp.dot(grad_attn, output_full, preferred_element_type=jnp.float32).astype(
        jnp.bfloat16
    )
    grad_blocks = lax.map(
        partial(attend_backward, score_scale=score_scale),
        (seq_blocks, grad_mixed.reshape(seq_count, SEQ_LEN, local_heads, HEAD_DIM), log_totals),
    )
    grad_proj = grad_blocks.reshape(group_tokens, 3, local_width)
    qkv_bias_grad = jnp.stack(
        [
            jnp.sum(grad_proj[:, 0].astype(jnp.float32), axis=0),
            jnp.sum(grad_proj[:, 2].astype(jnp.float32), axis=0),
        ]
    )
    qkv_grad = jnp.einsum("td,tcf->dcf", attn_in, grad_proj, preferred_element_type=jnp.float32)
    grad_attn_in = collect_grad(
        jnp.einsum("tcf,dcf->td", grad_proj, qkv_full, preferred_element_type=jnp.float32)
    )
    attn_resid_grad, attn_gain_grad, attn_shift_grad = norm_back(
        grad_attn_in, attn_hat, attn_inverse, attn_gain
    )
    input_grad = hidden_grad + attn_resid_grad
    qkv_sum, output_sum = in_one_piece(
        (qkv_grad.astype(jnp.bfloat16), output_grad.astype(jnp.bfloat16)), "row", 0, 1
    )
    bias_sums = lax.psum((qkv_bias_grad, up_bias_grad), "row")
    squares = jnp.stack(
        [
            jnp.sum(result * result),
            jnp.sum(attn_branch * attn_branch),
            jnp.sum(mlp_branch * mlp_branch),
        ]
    )
    stream_sums = lax.psum(
        (
            squares,
            attn_gain_grad,
            attn_shift_grad,
            output_bias_grad,
            mlp_gain_grad,
            mlp_shift_grad,
            down_bias_grad,
        ),
        ("row", "col"),
    )
    entry_count = local_tokens * lax.axis_size("row") * lax.axis_size("col") * width
    rms_values = jnp.sqrt(stream_sums[0] / entry_count)
    return (
        result.astype(jnp.bfloat16),
        input_grad,
        stream_sums[1],
        stream_sums[2],
        qkv_sum,
        bias_sums[0],
        output_sum,
        stream_sums[3],
        stream_sums[4],
        stream_sums[5],
        up_sum,
        bias_sums[1],
        down_sum,
        stream_sums[6],
        rms_values,
    )


def solution(mesh):
    placed = (
        P(("row", "col"), None),
        P(),
        P(),
        P("row", None, "col"),
        P(None, "col"),
        P("row", "col"),
        P(),
        P(),
        P(),
        P("row", "col"),
        P("col"),
        P("row", "col"),
        P(),
        P(("row", "col"), None),
    )
    return jax.shard_map(
        local,
        mesh=mesh,
        in_specs=placed,
        out_specs=(
            P(("row", "col"), None),
            P(("row", "col"), None),
            P(),
            P(),
            P("row", None, "col"),
            P(None, "col"),
            P("row", "col"),
            P(),
            P(),
            P(),
            P("row", "col"),
            P("col"),
            P("row", "col"),
            P(),
            P(),
        ),
        check_vma=False,
    )
```

profile of v0, /device:TPU:0, one launch (start us, length us, event | category | flops | bytes accessed | tf_op | source)
XLA Modules:
  0.0 694.7 jit_solution(2908344650220315940)
XLA Ops:
  10.9 2.4 fusion.44
  13.6 38.8 %all_gather.25 = bf16[768,3,192]{2,1,0:T(4,128)(2,1)S(1)} all-gather(bf16[96,3,192]{2,1,0:T(4,128)(2,1)S(1)} %copy.73), channel_id=1, replica_groups=mesh['row'=8,'col'=4] {'row'}, dimensions={0}, use_global_device_ids=true | all-gather | bytes 995328 | tf_op jit(solution)/shard_map/all_gather | solution.py:164
  54.5 31.2 %all_gather.26 = bf16[768,192]{1,0:T(8,128)(2,1)S(1)} all-gather(bf16[96,192]{1,0:T(8,128)(2,1)S(1)} %copy-done.23), channel_id=1, replica_groups=mesh['row'=8,'col'=4] {'row'}, dimensions={0}, use_global_device_ids=true | all-gather | bytes 331776 | tf_op jit(solution)/shard_map/all_gather | solution.py:165
  85.8 4.1 fusion.60
  90.2 3.0 reshape.189
  93.2 2.4 copy.75
  95.6 12.7 %while.22 = (s32[]{:T(128)}, bf16[2,1024,192]{1,2,0:T(8,128)(2,1)S(1)}, f32[2,3,1024]{2,1,0:T(4,128)}, bf16[2,1024,3,3,64]{1,4,3,2,0:T(8,128)(2,1)S(1)}, s32[]{:T(128)}) while((s32[]{:T(128)}, bf16[2,1024,192]{1,2,0:T(8,128)(2,1)S(1)}, f32[2,3,1024]{2,1,0:T(4,128)}, bf16[2,1024,3,3,64]{1,4,3,2,0:T(8,128)(2,1)S(1)}, s32[]{:T(128)}) %tuple.75), condition=%wide.region_5.6_spmd, body=%wide.region_2.5_spmd.sunk | while | flops 830665728 | bytes 42782856 | solution.py:178
  97.6 2.1 exponential_reduce_fusion.2
  99.7 2.2 fusion.98
  106.0 2.2 fusion.98
  109.2 3.7 fusion.61
  113.7 57.4 %reduce-scatter.9.cloned.1.call-done = f32[512,768]{1,0:T(8,128)} async-done(((f32[2048,768]{1,0:T(8,128)}), f32[512,768]{1,0:T(8,128)}) %reduce-scatter.9.cloned.1.call-update) | async-done | bytes 1572880 | tf_op jit(solution)/shard_map/reduce_scatter | solution.py:75
  171.0 2.5 fusion.58
  177.6 26.7 %all-gather.9.cloned.1.call-done = bf16[2048,768]{1,0:T(8,128)(2,1)} async-done(((bf16[512,768]{1,0:T(8,128)(2,1)}), bf16[2048,768]{1,0:T(8,128)(2,1)}) %all-gather.9.cloned.1.call-update) | async-done | bytes 3145744 | tf_op jit(solution)/shard_map/all_gather | solution.py:60
  204.3 7.5 %fusion.62 = f32[2048,768]{1,0:T(8,128)} fusion(bf16[2048,768]{1,0:T(8,128)(2,1)} %all-gather.9.cloned.1.call-done, bf16[768,768]{1,0:T(8,128)(2,1)} %all-gather.11.cloned.1.call-done), kind=kOutput, calls=%fused_computation.122 | convolution fusion | flops 2415919104 | bytes 10616832 | tf_op jit(solution)/shard_map/dot_general | solution.py:183
  211.8 36.3 %all-gather.13.cloned.1.call-done = bf16[768,768]{1,0:T(8,128)(2,1)} async-done(((bf16[96,768]{1,0:T(8,128)(2,1)}), bf16[768,768]{1,0:T(8,128)(2,1)}) %all-gather.13.cloned.1.call-update) | async-done | bytes 1179664 | tf_op jit(solution)/shard_map/all_gather | solution.py:169
  248.2 28.6 %all-gather.15.cloned.1.call-done = bf16[2048,768]{1,0:T(8,128)(2,1)} async-done(((bf16[512,768]{1,0:T(8,128)(2,1)}), bf16[2048,768]{1,0:T(8,128)(2,1)}) %all-gather.15.cloned.1.call-update) | async-done | bytes 3145744 | tf_op jit(solution)/shard_map/all_gather | solution.py:79
  276.7 9.8 %convert_reduce_fusion = (f32[768]{0:T(1024)}, bf16[2048,768]{1,0:T(8,128)(2,1)S(1)}) fusion(f32[2048,768]{1,0:T(8,128)} %fusion.62, f32[768]{0:T(1024)S(1)} %copy-done.36, bf16[2048,768]{1,0:T(8,128)(2,1)} %all-gather.15.cloned.1.call-done, bf16[768,768]{1,0:T(8,128)(2,1)} %all-gather.13.cloned.1.call-done), kind=kOutput, calls=%fused_computation.52 | convolution fusion | flops 2452094208 | bytes 13768704 | tf_op jit(solution)/shard_map/dot_general | solution.py:191
  288.3 4.0 convolution_convert_fusion
  292.3 10.0 %fusion.56 = f32[2048,768]{1,0:T(8,128)} fusion(bf16[768,768]{1,0:T(8,128)(2,1)} %all-gather.13.cloned.1.call-done, f32[2048,768]{1,0:T(8,128)} %fusion.62, f32[768]{0:T(1024)S(1)} %copy-done.36), kind=kOutput, calls=%fused_computation.117 | convolution fusion | flops 2431647744 | bytes 13765632 | tf_op jit(solution)/shard_map/dot_general | solution.py:39
  302.4 27.8 %reduce-scatter.13.cloned.1.call-done = bf16[512,768]{1,0:T(8,128)(2,1)} async-done(((bf16[2048,768]{1,0:T(8,128)(2,1)}), bf16[512,768]{1,0:T(8,128)(2,1)}) %reduce-scatter.13.cloned.1.call-update) | async-done | bytes 786448 | tf_op jit(solution)/shard_map/reduce_scatter | solution.py:83
  330.2 60.8 %reduce-scatter.11.cloned.1.call-done = f32[512,768]{1,0:T(8,128)} async-done(((f32[2048,768]{1,0:T(8,128)}), f32[512,768]{1,0:T(8,128)}) %reduce-scatter.11.cloned.1.call-update) | async-done | bytes 1572880 | tf_op jit(solution)/shard_map/reduce_scatter | solution.py:75
  391.0 4.8 multiply_reduce_fusion.4
  395.9 2.8 convert_reduce_fusion.6
  398.8 28.6 %all-gather.17.cloned.1.call-done = bf16[2048,768]{1,0:T(8,128)(2,1)} async-done(((bf16[512,768]{1,0:T(8,128)(2,1)}), bf16[2048,768]{1,0:T(8,128)(2,1)}) %all-gather.17.cloned.1.call-update) | async-done | bytes 3145744 | tf_op jit(solution)/shard_map/all_gather | solution.py:79
  427.4 3.1 convolution_convert_fusion.1
  433.3 45.2 %while.23 = (s32[]{:T(128)}, bf16[2,1024,3,3,64]{1,4,3,2,0:T(8,128)(2,1)}, bf16[2,1024,3,3,64]{1,4,3,2,0:T(8,128)(2,1)S(1)}, f32[2,3,1024]{2,1,0:T(4,128)S(1)}, bf16[2,1024,3,64]{1,3,2,0:T(8,128)(2,1)S(1)}, /*index=5*/s32[]{:T(128)}) while((s32[]{:T(128)}, bf16[2,1024,3,3,64]{1,4,3,2,0:T(8,128)(2,1)}, ...), condition=%wide.region_15.16_spmd, body=%wide.region_13.15_spmd.sunk | while | flops 2055533568 | bytes 155021600 | solution.py:211
  435.4 3.0 fusion.104
  438.5 4.0 multiply_reduce_fusion.9
  442.5 5.2 multiply_convert_fusion.5
  447.7 4.2 fusion.106
  458.0 3.0 fusion.104
  461.0 4.0 multiply_reduce_fusion.9
  465.0 5.2 multiply_convert_fusion.5
  470.2 4.2 fusion.106
  478.5 4.1 copy.79
  482.6 3.1 reshape.192
  485.8 6.0 bitcast_convert_fusion
  492.5 8.7 %convolution_bitcast_fusion = f32[768,768]{0,1:T(8,128)} fusion(bf16[2048,768]{1,0:T(8,128)(2,1)} %all-gather.15.cloned.1.call-done, f32[2048,768]{1,0:T(8,128)} %fusion.62, f32[768]{0:T(1024)S(1)} %copy-done.37), kind=kOutput, calls=%fused_computation.79 | convolution fusion | flops 2431647744 | bytes 11799552 | tf_op jit(solution)/shard_map/dot_general | solution.py:45
  501.2 3.2 copy.89
  504.5 6.9 fusion.63
  512.5 2.7 convolution_convert_fusion.2
  523.8 5.6 all-to-all-start
  529.4 2.5 pad_maximum_fusion.3
  533.7 39.7 %all-reduce.1 = (f32[2,192]{1,0:T(2,128)}, f32[768]{0:T(1024)}) all-reduce(f32[2,192]{1,0:T(2,128)S(1)} %pad_maximum_fusion.2, f32[768]{0:T(1024)S(1)} %copy-done.31), channel_id=1, replica_groups=mesh['row'=8,'col'=4] {'row'}, use_global_device_ids=true, to_apply=%region_26.27 | all-reduce | flops 1152 | bytes 9216 | tf_op jit(solution)/shard_map/psum | solution.py:233
  577.3 47.8 %all-reduce = (f32[768]{0:T(1024)}, f32[768]{0:T(1024)}, f32[768]{0:T(1024)}, f32[768]{0:T(1024)}, f32[768]{0:T(1024)}, /*index=5*/f32[768]{0:T(1024)}, f32[3]{0:T(128)S(1)}) all-reduce(f32[768]{0:T(1024)S(1)} %get-tuple-element.170, f32[768]{0:T(1024)S(1)} %get-tuple-element.177, ...), channel_id=1, replica_groups=mesh['row'=8,'col'=4] {'row','col'}, use_global_device_ids=true, to_apply=%region_20.21 | all-reduce | flops 4611 | bytes 36888 | tf_op jit(solution)/shard_map/psum | solution.py:241
  625.7 2.8 fusion.47
  628.5 58.4 %reduce-scatter.17.cloned.1.call-done = f32[96,768]{1,0:T(8,128)} async-done(((f32[768,768]{1,0:T(8,128)}), f32[96,768]{1,0:T(8,128)}) %reduce-scatter.17.cloned.1.call-update) | async-done | bytes 294928 | tf_op jit(solution)/shard_map/reduce_scatter | solution.py:200
  (181 shorter events, 50.7 us)
Async XLA Ops:
  8.0 5.4 copy-start.20
  8.0 77.7 %all-gather.7.cloned.1.call-start = ((), (), s32[]{:S(2)}) async-start(), calls=%async_computation.7 | async-start | bytes 3932160 | tf_op jit(solution)/shard_map/all_gather | solution.py:60
  9.4 43.0 %copy-start.21 = (f32[512]{0:T(512)}, f32[512]{0:T(512)S(1)}, u32[]{:S(2)}) copy-start(f32[512]{0:T(512)S(1)} %broadcast_multiply_fusion.5) | copy-start | bytes 6148
  10.9 2.4 copy-start.26
  13.4 41.2 %copy-start.23 = (bf16[96,192]{1,0:T(8,128)(2,1)S(1)}, bf16[96,192]{1,0:T(8,128)(2,1)}, u32[]{:S(2)}) copy-start(bf16[96,192]{1,0:T(8,128)(2,1)} %param.23) | copy-start | bytes 110596
  13.4 157.6 %reduce-scatter.9.cloned.1.call-start = ((), (), s32[]{:S(2)}) async-start(), calls=%async_computation.8 | async-start | bytes 7864320 | tf_op jit(solution)/shard_map/reduce_scatter | solution.py:75
  13.6 72.1 %copy-start.33 = (f32[2,192]{1,0:T(2,128)S(1)}, f32[2,192]{1,0:T(2,128)}, u32[]{:S(2)}) copy-start(f32[2,192]{1,0:T(2,128)} %param.22) | copy-start | bytes 4612
  97.5 2.1 copy-start.17
  99.7 2.2 copy-start.18
  103.9 2.1 copy-start.17
  106.0 2.2 copy-start.18
  113.0 58.0 %copy-start.6 = (bf16[512,768]{1,0:T(8,128)(2,1)S(1)}, bf16[512,768]{1,0:T(8,128)(2,1)}, u32[]{:S(2)}) copy-start(bf16[512,768]{1,0:T(8,128)(2,1)} %param.18) | copy-start | bytes 2359300
  113.0 58.0 %copy-start.29 = (f32[768]{0:T(1024)S(1)}, f32[768]{0:T(1024)}, u32[]{:S(2)}) copy-start(f32[768]{0:T(1024)} %param.24) | copy-start | bytes 9220
  113.0 64.6 %all-gather.11.cloned.1.call-start = ((), (), s32[]{:S(2)}) async-start(), calls=%async_computation.10 | async-start | bytes 1327104 | tf_op jit(solution)/shard_map/all_gather | solution.py:168
  113.6 61.1 %copy-start.24 = (f32[768]{0:T(1024)S(1)}, f32[768]{0:T(1024)}, u32[]{:S(2)}) copy-start(f32[768]{0:T(1024)} %param.25) | copy-start | bytes 9220
  113.6 61.0 %copy-start.30 = (f32[768]{0:T(1024)S(1)}, f32[768]{0:T(1024)}, u32[]{:S(2)}) copy-start(f32[768]{0:T(1024)} %param.26) | copy-start | bytes 9220
  113.6 90.7 %all-gather.9.cloned.1.call-start = ((), (), s32[]{:S(2)}) async-start(), calls=%async_computation.9 | async-start | bytes 3932160 | tf_op jit(solution)/shard_map/all_gather | solution.py:60
  175.9 72.3 %all-gather.13.cloned.1.call-start = ((), (), s32[]{:S(2)}) async-start(), calls=%async_computation.11 | async-start | bytes 1327104 | tf_op jit(solution)/shard_map/all_gather | solution.py:169
  176.4 100.3 %all-gather.15.cloned.1.call-start = ((), (), s32[]{:S(2)}) async-start(), calls=%async_computation.13 | async-start | bytes 3932160 | tf_op jit(solution)/shard_map/all_gather | solution.py:79
  177.2 99.6 %copy-start.36 = (f32[768]{0:T(1024)S(1)}, f32[768]{0:T(1024)}, u32[]{:S(2)}) copy-start(f32[768]{0:T(1024)} %param.28) | copy-start | bytes 9220
  177.2 153.0 %reduce-scatter.13.cloned.1.call-start = ((), (), s32[]{:S(2)}) async-start(), calls=%async_computation.14 | async-start | bytes 3932160 | tf_op jit(solution)/shard_map/reduce_scatter | solution.py:83
  276.7 11.5 %copy-start.35 = (bf16[768,768]{1,0:T(8,128)(2,1)S(1)}, bf16[768,768]{1,0:T(8,128)(2,1)}, u32[]{:S(2)}) copy-start(bf16[768,768]{1,0:T(8,128)(2,1)} %all-gather.11.cloned.1.call-done) | copy-start | bytes 3538948
  292.3 98.8 %reduce-scatter.11.cloned.1.call-start = ((), (), s32[]{:S(2)}) async-start(), calls=%async_computation.12 | async-start | bytes 7864320 | tf_op jit(solution)/shard_map/reduce_scatter | solution.py:75
  302.3 88.7 %copy-start.32 = (f32[768]{0:T(1024)S(1)}, f32[768]{0:T(1024)}, u32[]{:S(2)}) copy-start(f32[768]{0:T(1024)} %param.30) | copy-start | bytes 9220
  302.3 93.5 %copy-start.11 = (bf16[512,768]{1,0:T(8,128)(2,1)S(1)}, bf16[512,768]{1,0:T(8,128)(2,1)}, u32[]{:S(2)}) copy-start(bf16[512,768]{1,0:T(8,128)(2,1)} %param.31) | copy-start | bytes 2359300
  302.3 125.0 %all-gather.17.cloned.1.call-start = ((), (), s32[]{:S(2)}) async-start(), calls=%async_computation.15 | async-start | bytes 3932160 | tf_op jit(solution)/shard_map/all_gather | solution.py:79
  391.0 4.8 copy-start.2
  391.0 4.8 copy-start.12
  398.7 176.6 %reduce-scatter.15.cloned.1.call-start = ((), (), s32[]{:S(2)}) async-start(), calls=%async_computation.16 | async-start | bytes 3932160 | tf_op jit(solution)/shard_map/reduce_scatter | solution.py:83
  430.5 2.8 copy-start.19
  433.5 2.0 copy-start.4
  447.7 4.6 copy-start
  452.3 2.0 copy-start.3
  452.3 2.0 copy-start.13
  470.2 4.6 copy-start
  474.8 2.0 copy-start.3
  474.8 2.0 copy-start.13
  482.6 3.2 copy-start.16
  491.8 136.7 %reduce-scatter.19.cloned.1.call-start = ((), (), s32[]{:S(2)}) async-start(), calls=%async_computation.18 | async-start | bytes 2654208
  504.4 182.5 %reduce-scatter.17.cloned.1.call-start = ((), (), s32[]{:S(2)}) async-start(), calls=%async_computation.17 | async-start | bytes 2654208 | tf_op jit(solution)/shard_map/reduce_scatter | solution.py:200
  523.8 9.9 %copy-start.31 = (f32[768]{0:T(1024)S(1)}, f32[768]{0:T(1024)}, u32[]{:S(2)}) copy-start(f32[768]{0:T(1024)} %get-tuple-element.207) | copy-start | bytes 9220
  523.8 49.6 %all-to-all-start = ((bf16[8,96,768]{2,1,0:T(8,128)(2,1)}), bf16[8,96,768]{2,1,0:T(8,128)(2,1)S(1)}, u32[]{:S(2)}, u32[]{:S(2)}) async-start(bf16[8,96,768]{2,1,0:T(8,128)(2,1)} %copy.81), calls=%async_computation.4 | async-start | bytes 2359296 | tf_op jit(solution)/shard_map/all_to_all | solution.py:24
  532.0 43.4 %copy-start.7 = (bf16[512,768]{1,0:T(8,128)(2,1)S(1)}, bf16[512,768]{1,0:T(8,128)(2,1)}, u32[]{:S(2)}) copy-start(bf16[512,768]{1,0:T(8,128)(2,1)} %param.18) | copy-start | bytes 2359300
  532.0 43.4 %copy-start.22 = (f32[512]{0:T(512)S(1)}, f32[512]{0:T(512)}, u32[]{:S(2)}) copy-start(f32[512]{0:T(512)} %copy-done.21) | copy-start | bytes 6148
  532.0 43.4 %copy-start.25 = (f32[768]{0:T(1024)S(1)}, f32[768]{0:T(1024)}, u32[]{:S(2)}) copy-start(f32[768]{0:T(1024)} %param.19) | copy-start | bytes 9220
  532.0 43.4 %copy-start.27 = (f32[512]{0:T(512)S(1)}, f32[512]{0:T(512)}, u32[]{:S(2)}) copy-start(f32[512]{0:T(512)} %copy-done.26) | copy-start | bytes 6148
  573.4 3.9 copy-start.28
  573.4 52.3 %copy-start.10 = (f32[512,768]{1,0:T(8,128)S(1)}, f32[512,768]{1,0:T(8,128)}, u32[]{:S(2)}) copy-start(f32[512,768]{1,0:T(8,128)} %get-tuple-element.211) | copy-start | bytes 4718596
  (12 other events, 17.2 us)
Sparse Core Ops, SparseCore 0:
  13.5 31.2 all-gather.6
  113.1 57.8 reduce-scatter.8
  398.8 28.5 all-gather.16
  491.9 37.9 reduce-scatter.14
  533.8 80.8 reduce-scatter.18
  618.6 68.2 reduce-scatter.16
Sparse Core Ops, SparseCore 1:
  115.9 40.9 all-gather.10
  175.9 28.3 all-gather.8
  206.6 41.5 all-gather.12
  249.8 26.8 all-gather.14
  292.4 37.8 reduce-scatter.12
  332.8 58.2 reduce-scatter.10
where the time goes:
time: 705 us; the launch traced here: 695 us
  waiting for transfers between devices  327 us (46%)
  blocking collectives  157 us (22%)
  matrix products  107 us (15%)
  other arithmetic  42.2 us (6%)
  local copies, waits for them, and re-layouts  38.4 us (5%)
  between operations  16.4 us (2%)
    reduce_scatter x2, waiting for transfers between devices, branch_total(): lax.psum_scatter(partial_rows, 'col', scatter_dimension=0, tiled=True)  118 us
    reduce_scatter x1, waiting for transfers between devices, local(): lax.psum_scatter(up_grad, 'row', scatter_dimension=0, tiled=True)  58.4 us
    all_gather x2, waiting for transfers between devices, spread_grad(): return lax.all_gather(grad_rows, 'col', axis=0, tiled=True)  57.2 us
    psum x1, blocking collectives, local(): lax.psum((squares, attn_gain_grad, attn_shift_grad, output_bias_grad, mlp...  47.8 us
    psum x1, blocking collectives, local(): bias_sums = lax.psum((qkv_bias_grad, up_bias_grad), 'row')  39.7 us
    all_gather x1, blocking collectives, local(): lax.all_gather(qkv_weight, 'row', axis=0, tiled=True)  38.8 us
    all_gather x1, waiting for transfers between devices, local(): lax.all_gather(down_weight, 'row', axis=0, tiled=True)  36.3 us
    all_gather x1, blocking collectives, local(): lax.all_gather(output_weight, 'row', axis=0, tiled=True)  31.2 us
  transfers between devices with their start and end apart: 13, of which 8 were waited for; matrix products, arithmetic and copies ran while one was open for 9% of the time, Pallas kernels for 0%

commit v1 on v0

v1 whole, which is shorter than its diff:
```python
import math

import jax
import jax.numpy as jnp
from jax import lax
from jax.experimental import pallas as pl
from jax.experimental.pallas import tpu as pltpu
from jax.sharding import Mesh, PartitionSpec as P

HEAD_DIM = 64
EPSILON = 1e-06
SWAP = [(0, 1), (1, 0)]
LOG2E = math.log2(math.e)
BF16 = jnp.bfloat16
F32 = jnp.float32


def swap(array, axis):
    return lax.ppermute(array, axis, SWAP)


def dot_nn(left, right):
    return lax.dot_general(left, right, (((1,), (0,)), ((), ())), preferred_element_type=F32)


def dot_nt(left, right):
    return lax.dot_general(left, right, (((1,), (1,)), ((), ())), preferred_element_type=F32)


def dot_tn(left, right):
    return lax.dot_general(left, right, (((0,), (0,)), ((), ())), preferred_element_type=F32)


def xor_exchange(blocks_of, axes):
    got = {}
    count = len(axes)
    sizes = [2] * count
    for bits in range(1, 2**count):
        perm = [(i, i ^ bits) for i in range(math.prod(sizes))]
        got[bits] = lax.ppermute(blocks_of(bits), axes, perm)
    return got


def in_order(own, got, axes):
    parts = [own] + [got[bits] for bits in range(1, 2 ** len(axes))]
    for depth, axis in enumerate(reversed(axes)):
        bit = 2**depth
        flip = lax.axis_index(axis) == 1
        parts = [jnp.where(flip, parts[i ^ bit], parts[i]) for i in range(len(parts))]
    return jnp.stack(parts)


def pair_in_order(own, other, axis, dim):
    flip = lax.axis_index(axis) == 1
    return jnp.stack([jnp.where(flip, other, own), jnp.where(flip, own, other)], axis=dim)


def gather_rows(shard, rows):
    low, high = rows[-1], rows[:-1]
    n, c = shard.shape
    near = high[-2:]
    stack = in_order(shard, xor_exchange(lambda bits: shard, near), near)
    for axis in reversed(high[:-2]):
        other = swap(stack, axis)
        stack = pair_in_order(stack, other, axis, 0).reshape(-1, n, c)
    half = c // 2
    first, second = stack[:, :, :half], stack[:, :, half:]
    first_low, second_y = swap(first, low), swap(second, "y")
    first = pair_in_order(first, first_low, low, 1).reshape(-1, half)
    first_y = swap(first, "y")
    second_low = swap(jnp.stack([second, second_y]), low)
    second_own = pair_in_order(second, second_low[0], low, 1).reshape(-1, half)
    second_other = pair_in_order(second_y, second_low[1], low, 1).reshape(-1, half)
    return (
        jnp.concatenate([first, second_own], axis=1),
        jnp.concatenate([first_y, second_other], axis=1),
    )


def pick(array, axis, dim, other):
    zero = lax.index_in_dim(array, 0, dim, keepdims=False)
    one = lax.index_in_dim(array, 1, dim, keepdims=False)
    flip = lax.axis_index(axis) == (0 if other else 1)
    return jnp.where(flip, one, zero)


def scatter_rows(own, other, rows):
    low, high = rows[-1], rows[:-1]
    near = high[-2:]
    total = 2 ** len(rows)
    n, c = own.shape[0] // total, own.shape[1]
    half = c // 2
    own = own.reshape(total // 2, 2, n, c)
    other = other.reshape(total // 2, 2, n, c)
    a_own, a_other = own[..., :half], other[..., :half]
    b_own, b_other = own[..., half:], other[..., half:]
    a_got = swap(a_other, "y")
    b_send = jnp.stack([pick(b_own, low, 1, True), pick(b_other, low, 1, True)])
    b_got = swap(b_send, low)
    a_sum = a_own.astype(F32) + a_got.astype(F32)
    a_send = pick(a_sum, low, 1, True).astype(BF16)
    b_own = pick(b_own, low, 1, False).astype(F32) + b_got[0].astype(F32)
    b_other = (pick(b_other, low, 1, False).astype(F32) + b_got[1].astype(F32)).astype(BF16)
    a_got = swap(a_send, low)
    b_got = swap(b_other, "y")
    a_sum = pick(a_sum, low, 1, False) + a_got.astype(F32)
    b_sum = b_own + b_got.astype(F32)
    both = jnp.concatenate([a_sum, b_sum], axis=2)
    for axis in high[:-2]:
        both = both.reshape(2, -1, n, c)
        got = swap(pick(both, axis, 0, True).astype(BF16), axis)
        both = pick(both, axis, 0, False) + got.astype(F32)
    low_both = both.astype(BF16)
    place = lax.axis_index(near)
    take = lambda bits: lax.dynamic_index_in_dim(low_both, place ^ bits, 0, keepdims=False)
    got = xor_exchange(take, near)
    out = lax.dynamic_index_in_dim(both, place, 0, keepdims=False)
    for piece in got.values():
        out = out + piece.astype(F32)
    return out


def attend_forward_kernel(
    xa_ref, xb_ref, wa_ref, wb_ref, bias_ref, q_ref, k_ref, v_ref, mixed_ref, lse_ref, vt_ref
):
    step = pl.program_id(0)
    block = mixed_ref.shape[0]
    d = HEAD_DIM

    @pl.when(step == 0)
    def _():
        parts = []
        for kind in range(3):
            parts += [wa_ref[:, kind * d : (kind + 1) * d], wb_ref[:, kind * d : (kind + 1) * d]]
        weight = jnp.concatenate(parts, axis=1)
        rows = xa_ref.shape[0]
        for side, ref in enumerate((xa_ref, xb_ref)):
            proj = (dot_nn(ref[...], weight) + bias_ref[0:1, :]).astype(BF16)
            q_ref[side * rows : (side + 1) * rows, :] = proj[:, : 2 * d]
            k_ref[side * rows : (side + 1) * rows, :] = proj[:, 2 * d : 4 * d]
            v_ref[side * rows : (side + 1) * rows, :] = proj[:, 4 * d :]
        vt = v_ref[...].T
        for head in range(2):
            vt_ref[head, :d, :] = vt[head * d : (head + 1) * d, :]
            vt_ref[head, d:, :] = jnp.ones((vt_ref.shape[1] - d, vt.shape[1]), BF16)

    query = q_ref[pl.ds(pl.multiple_of(step * block, block), block), :]
    lane = lax.broadcasted_iota(jnp.int32, query.shape, 1)
    outs = []
    for head in range(2):
        masked = jnp.where(lane // d == head, query, jnp.zeros_like(query)) * BF16(d**-0.5)
        scores = dot_nt(k_ref[...], masked)
        top = jnp.max(scores, axis=0, keepdims=True)
        weights = jnp.exp2((scores - top) * LOG2E).astype(BF16)
        out = dot_nn(vt_ref[head], weights)
        total = out[d : d + 1, :]
        outs.append(out[:d, :] / total)
        lse_ref[head : head + 1, :] = top + jnp.log(total)
    mixed_ref[...] = jnp.concatenate(outs, axis=0).T.astype(BF16)


def attend_forward(xa, xb, wa, wb, bias):
    seq = xa.shape[0] * 2
    width = xa.shape[1]
    block = 256
    two = 2 * HEAD_DIM
    whole = lambda shape: pl.BlockSpec(shape, lambda i: (0,) * len(shape))
    out = jax.ShapeDtypeStruct((seq, two), BF16)
    return pl.pallas_call(
        attend_forward_kernel,
        grid=(seq // block,),
        in_specs=[
            whole(xa.shape),
            whole(xb.shape),
            whole(wa.shape),
            whole(wb.shape),
            whole(bias.shape),
        ],
        out_specs=[
            whole((seq, two)),
            whole((seq, two)),
            whole((seq, two)),
            pl.BlockSpec((block, two), lambda i: (i, 0)),
            pl.BlockSpec((8, block), lambda i: (0, i)),
        ],
        out_shape=[out, out, out, out, jax.ShapeDtypeStruct((8, seq), F32)],
        scratch_shapes=[pltpu.VMEM((2, HEAD_DIM + 16, seq), BF16)],
        cost_estimate=pl.CostEstimate(
            flops=2 * seq * width * 3 * two + 4 * seq * seq * two * 2,
            bytes_accessed=8 * seq * two * 4,
            transcendentals=2 * seq * seq,
        ),
        name="attend_forward",
    )(xa, xb, wa, wb, bias)


def attend_backward_kernel(
    q_ref, k_ref, v_ref, grad_ref, mixed_ref, lse_ref, dq_ref, dk_ref, dv_ref, kt_ref, dk_acc, dv_acc
):
    step = pl.program_id(0)
    d = HEAD_DIM
    scale = d**-0.5

    @pl.when(step == 0)
    def _():
        kt_ref[...] = k_ref[...].T
        dk_acc[...] = jnp.zeros_like(dk_acc)
        dv_acc[...] = jnp.zeros_like(dv_acc)

    query = q_ref[...]
    grad = grad_ref[...]
    lane = lax.broadcasted_iota(jnp.int32, query.shape, 1)
    dots = (grad.astype(F32) * mixed_ref[...].astype(F32)).T
    dqs = []
    for head in range(2):
        mine = lane // d == head
        query_h = jnp.where(mine, query, jnp.zeros_like(query))
        grad_h = jnp.where(mine, grad, jnp.zeros_like(grad))
        row_dots = jnp.sum(dots[head * d : (head + 1) * d, :], axis=0, keepdims=True)
        log_total = lse_ref[head : head + 1, :] * LOG2E
        scores = dot_nt(k_ref[...], query_h * BF16(scale))
        probs = jnp.exp2(scores * LOG2E - log_total)
        grad_probs = dot_nt(v_ref[...], grad_h)
        grad_scores = (probs * (grad_probs - row_dots)).astype(BF16)
        dv_acc[...] += dot_nn(probs.astype(BF16), grad_h)
        dk_acc[...] += dot_nn(grad_scores, query_h)
        dqs.append(dot_nn(kt_ref[head * d : (head + 1) * d, :], grad_scores) * scale)
    dq_ref[...] = jnp.concatenate(dqs, axis=0).T.astype(BF16)

    @pl.when(step == pl.num_programs(0) - 1)
    def _():
        dk_ref[...] = (dk_acc[...] * scale).astype(BF16)
        dv_ref[...] = dv_acc[...].astype(BF16)


def attend_backward(q, k, v, grad, mixed, lse):
    seq, two = q.shape
    block = 256
    whole = pl.BlockSpec((seq, two), lambda i: (0, 0))
    part = pl.BlockSpec((block, two), lambda i: (i, 0))
    out = jax.ShapeDtypeStruct((seq, two), BF16)
    return pl.pallas_call(
        attend_backward_kernel,
        grid=(seq // block,),
        in_specs=[part, whole, whole, part, part, pl.BlockSpec((8, block), lambda i: (0, i))],
        out_specs=[part, whole, whole],
        out_shape=[out, out, out],
        scratch_shapes=[
            pltpu.VMEM((two, seq), BF16),
            pltpu.VMEM((seq, two), F32),
            pltpu.VMEM((seq, two), F32),
        ],
        cost_estimate=pl.CostEstimate(
            flops=10 * seq * seq * two * 2,
            bytes_accessed=8 * seq * two * 2,
            transcendentals=2 * seq * seq,
        ),
        name="attend_backward",
    )(q, k, v, grad, mixed, lse)


def norm(resid, gain, shift):
    mean = jnp.mean(resid, axis=1, keepdims=True)
    centered = resid - mean
    inverse = lax.rsqrt(jnp.mean(jnp.square(centered), axis=1, keepdims=True) + EPSILON)
    hat = centered * inverse
    return (hat * gain + shift).astype(BF16), hat, inverse


def norm_back(grad, hat, inverse, gain):
    gain_grad = jnp.sum(grad * hat, axis=0)
    shift_grad = jnp.sum(grad, axis=0)
    grad_hat = grad * gain
    first = jnp.mean(grad_hat, axis=1, keepdims=True)
    second = jnp.mean(grad_hat * hat, axis=1, keepdims=True)
    return inverse * (grad_hat - first - hat * second), gain_grad, shift_grad


def gelu_tanh(values):
    return jax.nn.gelu(values, approximate=True)


def from_core_pair(own, other):
    return own + swap(other.astype(BF16), "core").astype(F32)


def make_local(rows):
    def local(
        layer_input,
        attn_gain,
        attn_shift,
        qkv_weight,
        qkv_bias,
        output_weight,
        output_bias,
        mlp_gain,
        mlp_shift,
        up_weight,
        up_bias,
        down_weight,
        down_bias,
        cotangent,
    ):
        tokens, width = layer_input.shape
        shard_rows, _, shard_cols = qkv_weight.shape
        heads = shard_cols // HEAD_DIM
        ff = up_weight.shape[1]
        d = HEAD_DIM
        y = lax.axis_index("y")

        bias_pack = jnp.concatenate([qkv_bias.reshape(-1), up_bias])
        bias_other = swap(bias_pack, "y")
        qkv_bias_other = bias_other[: 2 * shard_cols].reshape(2, shard_cols)
        up_bias_other = bias_other[2 * shard_cols :]

        residual = layer_input.astype(F32)
        attn_in, attn_hat, attn_inverse = norm(residual, attn_gain, attn_shift)
        attn_in_other = swap(attn_in, "core")
        attn_all = jnp.concatenate([attn_in, attn_in_other])

        def chunk_shard(h):
            cols = slice(h * d, (h + 1) * d)
            return jnp.concatenate(
                [qkv_weight[:, k, cols] for k in range(3)] + [output_weight[:, cols]], axis=1
            )

        chunks = [gather_rows(chunk_shard(h), rows) for h in range(heads)]
        up_own, up_other = gather_rows(up_weight, rows)
        down_own, down_other = gather_rows(down_weight, rows)
        cot_other = swap(cotangent, "core")
        grad_mlp = jnp.concatenate([cotangent, cot_other])

        attended = []
        zeros = jnp.zeros((d,), F32)
        for h in range(heads):
            cols = slice(h * d, (h + 1) * d)
            bias = jnp.concatenate(
                [
                    qkv_bias[0, cols],
                    qkv_bias_other[0, cols],
                    zeros,
                    zeros,
                    qkv_bias[1, cols],
                    qkv_bias_other[1, cols],
                ]
            )
            bias = jnp.broadcast_to(bias, (8, 6 * d))
            attended.append(attend_forward(attn_in, attn_in_other, *chunks[h], bias))
        mixed = jnp.concatenate([a[3] for a in attended], axis=1)
        out_pairs = [jnp.concatenate([a[:, 3 * d :], b[:, 3 * d :]], axis=1) for a, b in chunks]
        out_full = jnp.concatenate(out_pairs, axis=1)
        branch = dot_nt(mixed, out_full)
        attn_branch = from_core_pair(branch[:tokens], branch[tokens:]) + output_bias
        hidden_resid = residual + attn_branch
        mlp_in, mlp_hat, mlp_inverse = norm(hidden_resid, mlp_gain, mlp_shift)
        mlp_all = jnp.concatenate([mlp_in, swap(mlp_in, "core")])

        acts, slopes = [], []
        for weight, bias in ((up_own, up_bias), (up_other, up_bias_other)):
            pre = dot_nn(mlp_all, weight) + bias
            act, pull = jax.vjp(gelu_tanh, pre)
            acts.append(act.astype(BF16))
            slopes.append(pull(jnp.ones_like(pre))[0].astype(BF16))
        down_grads = [dot_tn(grad_mlp, act).astype(BF16) for act in acts]
        down_grad = scatter_rows(*down_grads, rows)
        branch = dot_nt(acts[0], down_own) + dot_nt(acts[1], down_other)
        mlp_branch = from_core_pair(branch[:tokens], branch[tokens:]) + down_bias
        result = hidden_resid + mlp_branch

        grad_out = cotangent.astype(F32)
        down_bias_grad = jnp.sum(grad_out, axis=0)
        pres = [
            (dot_nn(grad_mlp, w) * slope.astype(F32)).astype(BF16)
            for w, slope in ((down_own, slopes[0]), (down_other, slopes[1]))
        ]
        up_bias_grads = [jnp.sum(p.astype(F32), axis=0) for p in pres]
        up_grads = [dot_tn(mlp_all, p).astype(BF16) for p in pres]
        up_grad = scatter_rows(*up_grads, rows)
        back = dot_nt(pres[0], up_own) + dot_nt(pres[1], up_other)
        grad_mlp_in = from_core_pair(back[:tokens], back[tokens:])
        norm_grad, mlp_gain_grad, mlp_shift_grad = norm_back(
            grad_mlp_in, mlp_hat, mlp_inverse, mlp_gain
        )
        hidden_grad = grad_out + norm_grad
        grad_attn = hidden_grad.astype(BF16)
        output_bias_grad = jnp.sum(grad_attn.astype(F32), axis=0)
        grad_attn_all = jnp.concatenate([grad_attn, swap(grad_attn, "core")])
        output_grad = dot_tn(grad_attn_all, mixed).astype(BF16)
        grad_mixed = dot_nn(grad_attn_all, out_full).astype(BF16)

        back = 0.0
        attn_grads = []
        bias_grads = []
        for h in range(heads):
            q, k, v, mix, lse = attended[h]
            dq, dk, dv = attend_backward(
                q, k, v, grad_mixed[:, 2 * d * h : 2 * d * (h + 1)], mix, lse
            )
            bias_grads.append((jnp.sum(dq.astype(F32), axis=0), jnp.sum(dv.astype(F32), axis=0)))
            sides = []
            for side in range(2):
                cols = slice(side * d, (side + 1) * d)
                grad_proj = jnp.concatenate([dq[:, cols], dk[:, cols], dv[:, cols]], axis=1)
                back = back + dot_nt(grad_proj, chunks[h][side][:, : 3 * d])
                weight_grad = dot_tn(attn_all, grad_proj).astype(BF16)
                at = 2 * d * h + side * d
                sides.append(
                    jnp.concatenate([weight_grad, output_grad[:, at : at + d]], axis=1)
                )
            attn_grads.append(scatter_rows(*sides, rows))
        grad_attn_in = from_core_pair(back[:tokens], back[tokens:])
        norm_grad, attn_gain_grad, attn_shift_grad = norm_back(
            grad_attn_in, attn_hat, attn_inverse, attn_gain
        )
        input_grad = hidden_grad + norm_grad

        qkv_grad = jnp.stack(
            [
                jnp.concatenate([g[:, k * d : (k + 1) * d] for g in attn_grads], axis=1)
                for k in range(3)
            ],
            axis=1,
        )
        output_grad = jnp.concatenate([g[:, 3 * d :] for g in attn_grads], axis=1)

        squares = jnp.stack(
            [
                jnp.sum(result * result),
                jnp.sum(attn_branch * attn_branch),
                jnp.sum(mlp_branch * mlp_branch),
            ]
        )
        common = jnp.concatenate(
            [
                attn_gain_grad,
                attn_shift_grad,
                output_bias_grad,
                mlp_gain_grad,
                mlp_shift_grad,
                down_bias_grad,
                jnp.pad(squares, (0, 125)),
            ]
        )
        common = common + swap(common, "core")
        own = jnp.concatenate(
            [b[i][:d] for i in range(2) for b in bias_grads] + [up_bias_grads[0]]
        )
        other = jnp.concatenate(
            [b[i][d:] for i in range(2) for b in bias_grads] + [up_bias_grads[1]]
        )
        sums = jnp.concatenate([common, own])
        got = swap(jnp.concatenate([common, other]), "y")
        sums = sums + got
        for axis in reversed(rows):
            sums = sums + swap(sums, axis)
        entry_count = tokens * 2 ** (len(rows) + 2) * width
        vec = [sums[i * width : (i + 1) * width] for i in range(6)]
        rms_values = jnp.sqrt(sums[6 * width : 6 * width + 3] / entry_count)
        tail = sums[6 * width + 128 :]
        qkv_bias_grad = tail[: 2 * shard_cols].reshape(2, shard_cols)
        up_bias_grad = tail[2 * shard_cols :]
        return (
            result.astype(BF16),
            input_grad,
            vec[0],
            vec[1],
            qkv_grad,
            qkv_bias_grad,
            output_grad,
            vec[2],
            vec[3],
            vec[4],
            up_grad,
            up_bias_grad,
            down_grad,
            vec[5],
            rms_values,
        )

    return local


def solution(mesh):
    row_size, col_size = mesh.shape["row"], mesh.shape["col"]
    bits = row_size.bit_length() - 1
    rows = tuple(f"r{b}" for b in reversed(range(bits)))
    cube = Mesh(mesh.devices.reshape((2,) * bits + (col_size // 2, 2)), rows + ("y", "core"))
    col = ("y", "core")
    every = rows + col
    placed = (
        P(every, None),
        P(),
        P(),
        P(rows, None, col),
        P(None, col),
        P(rows, col),
        P(),
        P(),
        P(),
        P(rows, col),
        P(col),
        P(rows, col),
        P(),
        P(every, None),
    )
    return jax.shard_map(
        make_local(rows),
        mesh=cube,
        in_specs=placed,
        out_specs=(
            P(every, None),
            P(every, None),
            P(),
            P(),
            P(rows, None, col),
            P(None, col),
            P(rows, col),
            P(),
            P(),
            P(),
            P(rows, col),
            P(col),
            P(rows, col),
            P(),
            P(),
        ),
        check_vma=False,
    )
```

time: 705 us -> 456 us (0.65)
  waiting for transfers between devices: 327 us -> 95.2 us
  blocking collectives: 157 us -> 0 us
  starting transfers between devices: 6.49 us -> 97.2 us
  Pallas kernels: 0 us -> 55.2 us
  matrix products: 107 us -> 57.4 us
  local copies, waits for them, and re-layouts: 38.4 us -> 73.1 us
  other arithmetic: 42.2 us -> 68.8 us
  between operations: 16.4 us -> 2.69 us
    reduce_scatter x5 -> x0, waiting for transfers between devices: 204 us -> none  [the longest x2 118 us: branch_total(): lax.psum_scatter(partial_rows, 'col', scatter_dimension=0, tiled=True)]
    all_gather x6 -> x0, waiting for transfers between devices: 120 us -> none  [the longest x2 57.2 us: spread_grad(): return lax.all_gather(grad_rows, 'col', axis=0, tiled=True)]
    ppermute x0 -> x84, starting transfers between devices: none -> 97.2 us  [the longest x30 49.7 us: xor_exchange(): got[bits] = lax.ppermute(blocks_of(bits), axes, perm)]
    ppermute x0 -> x84, waiting for transfers between devices: none -> 95.2 us  [the longest x54 60.5 us: swap(): return lax.ppermute(array, axis, SWAP)]
    psum x2 -> x0, blocking collectives: 87.5 us -> none  [the longest x1 47.8 us: local(): lax.psum((squares, attn_gain_grad, attn_shift_grad, output_bias_grad, mlp...]
    all_gather x2 -> x0, blocking collectives: 70 us -> none  [the longest x1 38.8 us: local(): lax.all_gather(qkv_weight, 'row', axis=0, tiled=True)]
    pallas_call x0 -> x6, Pallas kernels: none -> 55.2 us  [the longest x3 30 us: attend_forward(): pl.pallas_call(attend_forward_kernel, grid=(seq // block,), in_specs=[who...]
    dot_general x24 -> x27, matrix products: 101 us -> 57.4 us  [the longest x11 24.9 us: dot_nt(): lax.dot_general(left, right, (((1,), (1,)), ((), ())), preferred_element_...]
  transfers between devices with their start and end apart: 13 -> 84, of which waited for: 8 -> 30; matrix products, arithmetic and copies ran while one was open for 9% -> 25% of each run, Pallas kernels for 0% -> 7%
where the time goes in v1:
time: 456 us; the launch traced here: 450 us
  starting transfers between devices  97.2 us (21%)
  waiting for transfers between devices  95.2 us (21%)
  local copies, waits for them, and re-layouts  73.1 us (16%)
  other arithmetic  68.8 us (15%)
  matrix products  57.4 us (13%)
  Pallas kernels  55.2 us (12%)
    ppermute x54, waiting for transfers between devices, swap(): return lax.ppermute(array, axis, SWAP)  60.5 us
    ppermute x30, starting transfers between devices, xor_exchange(): got[bits] = lax.ppermute(blocks_of(bits), axes, perm)  49.7 us
    ppermute x54, starting transfers between devices, swap(): return lax.ppermute(array, axis, SWAP)  47.5 us
    ppermute x30, waiting for transfers between devices, xor_exchange(): got[bits] = lax.ppermute(blocks_of(bits), axes, perm)  34.7 us
    pallas_call x3, Pallas kernels, attend_forward(): pl.pallas_call(attend_forward_kernel, grid=(seq // block,), in_specs=[who...  30 us
    pallas_call x3, Pallas kernels, attend_backward(): pl.pallas_call(attend_backward_kernel, grid=(seq // block,), in_specs=[pa...  25.2 us
    dot_general x11, matrix products, dot_nt(): lax.dot_general(left, right, (((1,), (1,)), ((), ())), preferred_element_...  24.9 us
    dot_general x11, matrix products, dot_tn(): lax.dot_general(left, right, (((0,), (0,)), ((), ())), preferred_element_...  20.1 us
  transfers between devices with their start and end apart: 84, of which 30 were waited for; matrix products, arithmetic and copies ran while one was open for 25% of the time, Pallas kernels for 7%

profile of v1, /device:TPU:0, one launch (start us, length us, event | category | flops | bytes accessed | tf_op | source)
XLA Modules:
  0.0 449.5 jit_solution(11997903422943747001)
XLA Ops:
  2.7 4.1 collective-permute-start.10
  17.5 2.5 collective-permute-start.18
  21.8 3.6 collective-permute-start.1
  26.2 3.6 collective-permute-start.25
  30.9 2.8 collective-permute-done.2
  35.6 8.1 %collective-permute-start.33 = (bf16[96,768]{1,0:T(8,128)(2,1)S(1)}, bf16[96,768]{1,0:T(8,128)(2,1)S(1)}, u32[]{:S(2)}, u32[]{:S(2)}) collective-permute-start(bf16[96,768]{1,0:T(8,128)(2,1)S(1)} %copy-done.63), channel_id=1, source_target_pairs={{0,8},{8,0},{16,24},{24,16},{1,9},{9,1},{17,25},{25,17},{2,10},{10... | collective-permute-start | bytes 442376 | tf_op jit(solution)/shard_map/ppermute | solution.py:40
  43.7 5.1 %collective-permute-done.26 = bf16[96,768]{1,0:T(8,128)(2,1)S(1)} collective-permute-done((bf16[96,768]{1,0:T(8,128)(2,1)S(1)}, bf16[96,768]{1,0:T(8,128)(2,1)S(1)}, u32[]{:S(2)}, u32[]{:S(2)}) %collective-permute-start.26) | collective-permute-done | bytes 147488 | tf_op jit(solution)/shard_map/ppermute | solution.py:40
  50.9 3.0 collective-permute-done.32
  63.8 4.1 collective-permute-done.21
  71.0 4.0 collective-permute-done.14
  84.9 2.5 concatenate.155
  99.6 9.9 %attend_forward.3 = (bf16[1024,128]{1,0:T(8,128)(2,1)}, bf16[1024,128]{1,0:T(8,128)(2,1)}, bf16[1024,128]{1,0:T(8,128)(2,1)}, bf16[1024,128]{1,0:T(8,128)(2,1)}, f32[8,1024]{1,0:T(8,128)}) custom-call(bf16[512,768]{1,0:T(8,128)(2,1)} %fusion.21.xa_ref, bf16[512,768]{1,0:T(8,128)(2,1)} %collective-permute-done.xb_ref, ...), custom_call_target="tpu_custom_call" | custom-call | flops 1677721600 | bytes 4194304 | tf_op jit(solution)/shard_map/attend_forward/pallas_call | solution.py:169
  111.8 9.9 %attend_forward.4 = (bf16[1024,128]{1,0:T(8,128)(2,1)}, bf16[1024,128]{1,0:T(8,128)(2,1)}, bf16[1024,128]{1,0:T(8,128)(2,1)}, bf16[1024,128]{1,0:T(8,128)(2,1)}, f32[8,1024]{1,0:T(8,128)}) custom-call(bf16[512,768]{1,0:T(8,128)(2,1)} %fusion.21.xa_ref, bf16[512,768]{1,0:T(8,128)(2,1)} %collective-permute-done.xb_ref, ...), custom_call_target="tpu_custom_call" | custom-call | flops 1677721600 | bytes 4194304 | tf_op jit(solution)/shard_map/attend_forward/pallas_call | solution.py:169
  124.1 10.2 %attend_forward.5 = (bf16[1024,128]{1,0:T(8,128)(2,1)}, bf16[1024,128]{1,0:T(8,128)(2,1)}, bf16[1024,128]{1,0:T(8,128)(2,1)}, bf16[1024,128]{1,0:T(8,128)(2,1)}, f32[8,1024]{1,0:T(8,128)}) custom-call(bf16[512,768]{1,0:T(8,128)(2,1)} %fusion.21.xa_ref, bf16[512,768]{1,0:T(8,128)(2,1)} %collective-permute-done.xb_ref, ...), custom_call_target="tpu_custom_call" | custom-call | flops 1677721600 | bytes 4194304 | tf_op jit(solution)/shard_map/attend_forward/pallas_call | solution.py:169
  136.0 2.3 fusion.155
  152.5 2.3 fusion.127
  158.1 11.5 %collective-permute-done.36 = bf16[2,4,96,384]{3,2,1,0:T(8,128)(2,1)S(1)} collective-permute-done((bf16[2,4,96,384]{3,2,1,0:T(8,128)(2,1)S(1)}, bf16[2,4,96,384]{3,2,1,0:T(8,128)(2,1)S(1)}, u32[]{:S(2)}, u32[]{:S(2)}) %collective-permute-start.36) | collective-permute-done | bytes 589856 | tf_op jit(solution)/shard_map/ppermute | solution.py:19
  176.2 9.8 %collective-permute-done.38 = bf16[768,384]{1,0:T(8,128)(2,1)S(1)} collective-permute-done((bf16[768,384]{1,0:T(8,128)(2,1)S(1)}, bf16[768,384]{1,0:T(8,128)(2,1)S(1)}, u32[]{:S(2)}, u32[]{:S(2)}) %collective-permute-start.38) | collective-permute-done | bytes 589856 | tf_op jit(solution)/shard_map/ppermute | solution.py:19
  186.0 4.3 convert_reduce_fusion
  194.9 4.3 convert_reduce_fusion.1
  199.2 2.1 fusion.34
  208.9 2.1 convolution_add_fusion.1
  212.8 5.0 %collective-permute-done.79 = bf16[2,4,96,384]{3,2,1,0:T(8,128)(2,1)S(1)} collective-permute-done((bf16[2,4,96,384]{3,2,1,0:T(8,128)(2,1)S(1)}, bf16[2,4,96,384]{3,2,1,0:T(8,128)(2,1)S(1)}, u32[]{:S(2)}, u32[]{:S(2)}) %collective-permute-start.79) | collective-permute-done | bytes 589856 | tf_op jit(solution)/shard_map/ppermute | solution.py:19
  220.6 7.7 %collective-permute-done.72 = bf16[2,4,96,384]{3,2,1,0:T(8,128)(2,1)S(1)} collective-permute-done((bf16[2,4,96,384]{3,2,1,0:T(8,128)(2,1)S(1)}, bf16[2,4,96,384]{3,2,1,0:T(8,128)(2,1)S(1)}, u32[]{:S(2)}, u32[]{:S(2)}) %collective-permute-start.72) | collective-permute-done | bytes 589856 | tf_op jit(solution)/shard_map/ppermute | solution.py:19
  229.1 2.2 collective-permute-done.70
  234.6 2.8 multiply_reduce_fusion.3
  237.4 2.5 convert_reduce_fusion.4
  240.4 2.6 collective-permute-start.82
  245.4 4.1 collective-permute-done.81
  249.5 4.9 %collective-permute-done.82 = bf16[96,768]{1,0:T(8,128)(2,1)S(1)} collective-permute-done((bf16[96,768]{1,0:T(8,128)(2,1)S(1)}, bf16[96,768]{1,0:T(8,128)(2,1)S(1)}, u32[]{:S(2)}, u32[]{:S(2)}) %collective-permute-start.82) | collective-permute-done | bytes 147488 | tf_op jit(solution)/shard_map/ppermute | solution.py:40
  257.2 9.8 %collective-permute-done.75 = bf16[96,768]{1,0:T(8,128)(2,1)S(1)} collective-permute-done((bf16[96,768]{1,0:T(8,128)(2,1)S(1)}, bf16[96,768]{1,0:T(8,128)(2,1)S(1)}, u32[]{:S(2)}, u32[]{:S(2)}) %collective-permute-start.75) | collective-permute-done | bytes 147488 | tf_op jit(solution)/shard_map/ppermute | solution.py:40
  269.8 8.3 %attend_backward.3 = (bf16[1024,128]{1,0:T(8,128)(2,1)}, bf16[1024,128]{1,0:T(8,128)(2,1)}, bf16[1024,128]{1,0:T(8,128)(2,1)}) custom-call(bf16[1024,128]{1,0:T(8,128)(2,1)} %get-tuple-element.42.q_ref, bf16[1024,128]{1,0:T(8,128)(2,1)} %get-tuple-element.43.k_ref, bf16[1024,128]{1,0:T(8,128)(2,1)} %get-tuple-element.44.v_ref, ...), custom_call_target="tpu_custom_call" | custom-call | flops 2684354560 | bytes 2097152 | tf_op jit(solution)/shard_map/attend_backward/pallas_call | solution.py:242
  284.4 2.1 convolution_convert_fusion.10
  292.5 8.3 %attend_backward.4 = (bf16[1024,128]{1,0:T(8,128)(2,1)}, bf16[1024,128]{1,0:T(8,128)(2,1)}, bf16[1024,128]{1,0:T(8,128)(2,1)}) custom-call(bf16[1024,128]{1,0:T(8,128)(2,1)} %get-tuple-element.49.q_ref, bf16[1024,128]{1,0:T(8,128)(2,1)} %get-tuple-element.50.k_ref, bf16[1024,128]{1,0:T(8,128)(2,1)} %get-tuple-element.51.v_ref, ...), custom_call_target="tpu_custom_call" | custom-call | flops 2684354560 | bytes 2097152 | tf_op jit(solution)/shard_map/attend_backward/pallas_call | solution.py:242
  305.4 2.2 convolution_convert_fusion.8
  313.6 8.5 %attend_backward.5 = (bf16[1024,128]{1,0:T(8,128)(2,1)}, bf16[1024,128]{1,0:T(8,128)(2,1)}, bf16[1024,128]{1,0:T(8,128)(2,1)}) custom-call(bf16[1024,128]{1,0:T(8,128)(2,1)} %get-tuple-element.56.q_ref, bf16[1024,128]{1,0:T(8,128)(2,1)} %get-tuple-element.57.k_ref, bf16[1024,128]{1,0:T(8,128)(2,1)} %get-tuple-element.58.v_ref, ...), custom_call_target="tpu_custom_call" | custom-call | flops 2684354560 | bytes 2097152 | tf_op jit(solution)/shard_map/attend_backward/pallas_call | solution.py:242
  326.7 2.2 convolution_convert_fusion.6
  342.0 2.3 fusion.56
  344.3 2.2 convolution_convert_fusion.11
  354.4 3.5 fusion.50
  357.9 2.2 convolution_convert_fusion.9
  369.1 3.5 fusion.44
  372.6 2.2 convolution_convert_fusion.7
  384.5 2.3 add_add_fusion
  404.4 3.3 collective-permute-start.53
  436.4 2.6 collective-permute-done.46
  439.7 3.1 collective-permute-done.47
  443.5 3.2 fusion.25
  (567 shorter events, 230.7 us)
Async XLA Ops:
  2.7 17.4 %collective-permute-start.10 = (bf16[96,256]{1,0:T(8,128)(2,1)S(1)}, bf16[96,256]{1,0:T(8,128)(2,1)S(1)}, u32[]{:S(2)}, u32[]{:S(2)}) collective-permute-start(bf16[96,256]{1,0:T(8,128)(2,1)S(1)} %pad_maximum_fusion.85), channel_id=1, source_target_pairs={{0,16},{8,24},{16,0},{24,8},{1,17},{9,25},{17,1},{25,9},{2,18},{10... | collective-permute-start | bytes 147464 | tf_op jit(solution)/shard_map/ppermute | solution.py:40
  6.8 15.0 %collective-permute-start.11 = (bf16[96,256]{1,0:T(8,128)(2,1)S(1)}, bf16[96,256]{1,0:T(8,128)(2,1)S(1)}, u32[]{:S(2)}, u32[]{:S(2)}) collective-permute-start(bf16[96,256]{1,0:T(8,128)(2,1)S(1)} %pad_maximum_fusion.85), channel_id=1, source_target_pairs={{0,8},{8,0},{16,24},{24,16},{1,9},{9,1},{17,25},{25,17},{2,10},{10... | collective-permute-start | bytes 147464 | tf_op jit(solution)/shard_map/ppermute | solution.py:40
  8.5 16.9 %collective-permute-start.16 = (bf16[96,256]{1,0:T(8,128)(2,1)S(1)}, bf16[96,256]{1,0:T(8,128)(2,1)S(1)}, u32[]{:S(2)}, u32[]{:S(2)}) collective-permute-start(bf16[96,256]{1,0:T(8,128)(2,1)S(1)} %pad_maximum_fusion.86), channel_id=1, source_target_pairs={{0,24},{8,16},{16,8},{24,0},{1,25},{9,17},{17,9},{25,1},{2,26},{10... | collective-permute-start | bytes 147464 | tf_op jit(solution)/shard_map/ppermute | solution.py:40
  8.5 16.9 %collective-permute-start.17 = (bf16[96,256]{1,0:T(8,128)(2,1)S(1)}, bf16[96,256]{1,0:T(8,128)(2,1)S(1)}, u32[]{:S(2)}, u32[]{:S(2)}) collective-permute-start(bf16[96,256]{1,0:T(8,128)(2,1)S(1)} %pad_maximum_fusion.86), channel_id=1, source_target_pairs={{0,16},{8,24},{16,0},{24,8},{1,17},{9,25},{17,1},{25,9},{2,18},{10... | collective-permute-start | bytes 147464 | tf_op jit(solution)/shard_map/ppermute | solution.py:40
  20.1 9.7 %collective-permute-start.9 = (bf16[96,256]{1,0:T(8,128)(2,1)S(1)}, bf16[96,256]{1,0:T(8,128)(2,1)S(1)}, u32[]{:S(2)}, u32[]{:S(2)}) collective-permute-start(bf16[96,256]{1,0:T(8,128)(2,1)S(1)} %pad_maximum_fusion.85), channel_id=1, source_target_pairs={{0,24},{8,16},{16,8},{24,0},{1,25},{9,17},{17,9},{25,1},{2,26},{10... | collective-permute-start | bytes 147464 | tf_op jit(solution)/shard_map/ppermute | solution.py:40
  29.8 19.1 %collective-permute-start.26 = (bf16[96,768]{1,0:T(8,128)(2,1)S(1)}, bf16[96,768]{1,0:T(8,128)(2,1)S(1)}, u32[]{:S(2)}, u32[]{:S(2)}) collective-permute-start(bf16[96,768]{1,0:T(8,128)(2,1)S(1)} %copy-done.62), channel_id=1, source_target_pairs={{0,16},{8,24},{16,0},{24,8},{1,17},{9,25},{17,1},{25,9},{2,18},{10... | collective-permute-start | bytes 442376 | tf_op jit(solution)/shard_map/ppermute | solution.py:40
  30.0 18.8 %collective-permute-start.27 = (bf16[96,768]{1,0:T(8,128)(2,1)S(1)}, bf16[96,768]{1,0:T(8,128)(2,1)S(1)}, u32[]{:S(2)}, u32[]{:S(2)}) collective-permute-start(bf16[96,768]{1,0:T(8,128)(2,1)S(1)} %copy-done.62), channel_id=1, source_target_pairs={{0,8},{8,0},{16,24},{24,16},{1,9},{9,1},{17,25},{25,17},{2,10},{10... | collective-permute-start | bytes 442376 | tf_op jit(solution)/shard_map/ppermute | solution.py:40
  33.7 16.8 %collective-permute-start.31 = (bf16[96,768]{1,0:T(8,128)(2,1)S(1)}, bf16[96,768]{1,0:T(8,128)(2,1)S(1)}, u32[]{:S(2)}, u32[]{:S(2)}) collective-permute-start(bf16[96,768]{1,0:T(8,128)(2,1)S(1)} %copy-done.63), channel_id=1, source_target_pairs={{0,24},{8,16},{16,8},{24,0},{1,25},{9,17},{17,9},{25,1},{2,26},{10... | collective-permute-start | bytes 442376 | tf_op jit(solution)/shard_map/ppermute | solution.py:40
  34.5 19.4 %collective-permute-start.32 = (bf16[96,768]{1,0:T(8,128)(2,1)S(1)}, bf16[96,768]{1,0:T(8,128)(2,1)S(1)}, u32[]{:S(2)}, u32[]{:S(2)}) collective-permute-start(bf16[96,768]{1,0:T(8,128)(2,1)S(1)} %copy-done.63), channel_id=1, source_target_pairs={{0,16},{8,24},{16,0},{24,8},{1,17},{9,25},{17,1},{25,9},{2,18},{10... | collective-permute-start | bytes 442376 | tf_op jit(solution)/shard_map/ppermute | solution.py:40
  35.6 19.8 %collective-permute-start.33 = (bf16[96,768]{1,0:T(8,128)(2,1)S(1)}, bf16[96,768]{1,0:T(8,128)(2,1)S(1)}, u32[]{:S(2)}, u32[]{:S(2)}) collective-permute-start(bf16[96,768]{1,0:T(8,128)(2,1)S(1)} %copy-done.63), channel_id=1, source_target_pairs={{0,8},{8,0},{16,24},{24,16},{1,9},{9,1},{17,25},{25,17},{2,10},{10... | collective-permute-start | bytes 442376 | tf_op jit(solution)/shard_map/ppermute | solution.py:40
  48.9 50.1 %collective-permute-start = (bf16[512,768]{1,0:T(8,128)(2,1)}, bf16[512,768]{1,0:T(8,128)(2,1)}, u32[]{:S(2)}, u32[]{:S(2)}) collective-permute-start(bf16[512,768]{1,0:T(8,128)(2,1)} %fusion.21.xa_ref), channel_id=1, source_target_pairs={{0,1},{1,0},{2,3},{3,2},{4,5},{5,4},{6,7},{7,6},{8,9},{9,8},{10,11... | collective-permute-start | bytes 2359304 | tf_op jit(solution)/shard_map/ppermute | solution.py:19
  48.9 97.3 %collective-permute-start.40 = (bf16[512,768]{1,0:T(8,128)(2,1)}, bf16[512,768]{1,0:T(8,128)(2,1)}, u32[]{:S(2)}, u32[]{:S(2)}) collective-permute-start(bf16[512,768]{1,0:T(8,128)(2,1)} %param.27), channel_id=1, source_target_pairs={{0,1},{1,0},{2,3},{3,2},{4,5},{5,4},{6,7},{7,6},{8,9},{9,8},{10,11... | collective-permute-start | bytes 2359304 | tf_op jit(solution)/shard_map/ppermute | solution.py:19
  62.2 14.7 %collective-permute-start.4 = (bf16[4,96,128]{2,1,0:T(8,128)(2,1)S(1)}, bf16[4,96,128]{2,1,0:T(8,128)(2,1)S(1)}, u32[]{:S(2)}, u32[]{:S(2)}) collective-permute-start(bf16[4,96,128]{2,1,0:T(8,128)(2,1)S(1)} %get-tuple-element.203), channel_id=1, source_target_pairs={{0,4},{4,0},{1,5},{5,1},{2,6},{6,2},{3,7},{7,3},{8,12},{12,8},{9,1... | collective-permute-start | bytes 294920 | tf_op jit(solution)/shard_map/ppermute | solution.py:19
  75.0 14.9 %collective-permute-start.29 = (bf16[4,96,384]{2,1,0:T(8,128)(2,1)}, bf16[4,96,384]{2,1,0:T(8,128)(2,1)}, u32[]{:S(2)}, u32[]{:S(2)}) collective-permute-start(bf16[4,96,384]{2,1,0:T(8,128)(2,1)} %get-tuple-element.120), channel_id=1, source_target_pairs={{0,2},{2,0},{1,3},{3,1},{4,6},{6,4},{5,7},{7,5},{8,10},{10,8},{9,1... | collective-permute-start | bytes 884744 | tf_op jit(solution)/shard_map/ppermute | solution.py:19
  76.9 66.9 %collective-permute-start.35 = (bf16[4,96,384]{2,1,0:T(8,128)(2,1)}, bf16[4,96,384]{2,1,0:T(8,128)(2,1)}, u32[]{:S(2)}, u32[]{:S(2)}) collective-permute-start(bf16[4,96,384]{2,1,0:T(8,128)(2,1)} %get-tuple-element.127), channel_id=1, source_target_pairs={{0,2},{2,0},{1,3},{3,1},{4,6},{6,4},{5,7},{7,5},{8,10},{10,8},{9,1... | collective-permute-start | bytes 884744 | tf_op jit(solution)/shard_map/ppermute | solution.py:19
  77.2 14.8 %collective-permute-start.22 = (bf16[768,128]{1,0:T(8,128)(2,1)S(1)}, bf16[768,128]{1,0:T(8,128)(2,1)}, u32[]{:S(2)}, u32[]{:S(2)}) collective-permute-start(bf16[768,128]{1,0:T(8,128)(2,1)S(1)} %bitcast.628), channel_id=1, source_target_pairs={{0,2},{2,0},{1,3},{3,1},{4,6},{6,4},{5,7},{7,5},{8,10},{10,8},{9,1... | collective-permute-start | bytes 589832 | tf_op jit(solution)/shard_map/ppermute | solution.py:19
  96.0 55.1 %collective-permute-start.30 = (bf16[2,4,96,384]{3,2,1,0:T(8,128)(2,1)}, bf16[2,4,96,384]{3,2,1,0:T(8,128)(2,1)}, u32[]{:S(2)}, u32[]{:S(2)}) collective-permute-start(bf16[2,4,96,384]{3,2,1,0:T(8,128)(2,1)} %pad_maximum_fusion.21), channel_id=1, source_target_pairs={{0,4},{4,0},{1,5},{5,1},{2,6},{6,2},{3,7},{7,3},{8,12},{12,8},{9,1... | collective-permute-start | bytes 1769480 | tf_op jit(solution)/shard_map/ppermute | solution.py:19
  141.0 11.5 %collective-permute-start.23 = (bf16[512,768]{1,0:T(8,128)(2,1)}, bf16[512,768]{1,0:T(8,128)(2,1)}, u32[]{:S(2)}, u32[]{:S(2)}) collective-permute-start(bf16[512,768]{1,0:T(8,128)(2,1)} %slice.1265), channel_id=1, source_target_pairs={{0,1},{1,0},{2,3},{3,2},{4,5},{5,4},{6,7},{7,6},{8,9},{9,8},{10,11... | collective-permute-start | bytes 2359304 | tf_op jit(solution)/shard_map/ppermute | solution.py:19
  141.0 10.1 %collective-permute-start.28 = (bf16[4,96,384]{2,1,0:T(8,128)(2,1)}, bf16[4,96,384]{2,1,0:T(8,128)(2,1)}, u32[]{:S(2)}, u32[]{:S(2)}) collective-permute-start(bf16[4,96,384]{2,1,0:T(8,128)(2,1)} %get-tuple-element.118), channel_id=1, source_target_pairs={{0,4},{4,0},{1,5},{5,1},{2,6},{6,2},{3,7},{7,3},{8,12},{12,8},{9,1... | collective-permute-start | bytes 884744 | tf_op jit(solution)/shard_map/ppermute | solution.py:19
  143.8 14.3 %collective-permute-start.34 = (bf16[4,96,384]{2,1,0:T(8,128)(2,1)}, bf16[4,96,384]{2,1,0:T(8,128)(2,1)S(1)}, u32[]{:S(2)}, u32[]{:S(2)}) collective-permute-start(bf16[4,96,384]{2,1,0:T(8,128)(2,1)} %get-tuple-element.125), channel_id=1, source_target_pairs={{0,4},{4,0},{1,5},{5,1},{2,6},{6,2},{3,7},{7,3},{8,12},{12,8},{9,1... | collective-permute-start | bytes 884744 | tf_op jit(solution)/shard_map/ppermute | solution.py:19
  146.2 23.4 %collective-permute-start.36 = (bf16[2,4,96,384]{3,2,1,0:T(8,128)(2,1)S(1)}, bf16[2,4,96,384]{3,2,1,0:T(8,128)(2,1)S(1)}, u32[]{:S(2)}, u32[]{:S(2)}) collective-permute-start(bf16[2,4,96,384]{3,2,1,0:T(8,128)(2,1)S(1)} %pad_maximum_fusion.25), channel_id=1, source_target_pairs={{0,4},{4,0},{1,5},{5,1},{2,6},{6,2},{3,7},{7,3},{8,12},{12,8},{9,1... | collective-permute-start | bytes 1769480 | tf_op jit(solution)/shard_map/ppermute | solution.py:19
  155.9 17.1 %collective-permute-start.24 = (bf16[512,768]{1,0:T(8,128)(2,1)S(1)}, bf16[512,768]{1,0:T(8,128)(2,1)S(1)}, u32[]{:S(2)}, u32[]{:S(2)}) collective-permute-start(bf16[512,768]{1,0:T(8,128)(2,1)S(1)} %add_convert_fusion), channel_id=1, source_target_pairs={{0,1},{1,0},{2,3},{3,2},{4,5},{5,4},{6,7},{7,6},{8,9},{9,8},{10,11... | collective-permute-start | bytes 2359304 | tf_op jit(solution)/shard_map/ppermute | solution.py:19
  156.0 16.9 %collective-permute-start.37 = (bf16[768,384]{1,0:T(8,128)(2,1)S(1)}, bf16[768,384]{1,0:T(8,128)(2,1)S(1)}, u32[]{:S(2)}, u32[]{:S(2)}) collective-permute-start(bf16[768,384]{1,0:T(8,128)(2,1)S(1)} %bitcast.638), channel_id=1, source_target_pairs={{0,2},{2,0},{1,3},{3,1},{4,6},{6,4},{5,7},{7,5},{8,10},{10,8},{9,1... | collective-permute-start | bytes 1769480 | tf_op jit(solution)/shard_map/ppermute | solution.py:19
  170.9 15.0 %collective-permute-start.38 = (bf16[768,384]{1,0:T(8,128)(2,1)S(1)}, bf16[768,384]{1,0:T(8,128)(2,1)S(1)}, u32[]{:S(2)}, u32[]{:S(2)}) collective-permute-start(bf16[768,384]{1,0:T(8,128)(2,1)S(1)} %bitcast.645), channel_id=1, source_target_pairs={{0,2},{2,0},{1,3},{3,1},{4,6},{6,4},{5,7},{7,5},{8,10},{10,8},{9,1... | collective-permute-start | bytes 1769480 | tf_op jit(solution)/shard_map/ppermute | solution.py:19
  201.5 16.3 %collective-permute-start.79 = (bf16[2,4,96,384]{3,2,1,0:T(8,128)(2,1)S(1)}, bf16[2,4,96,384]{3,2,1,0:T(8,128)(2,1)S(1)}, u32[]{:S(2)}, u32[]{:S(2)}) collective-permute-start(bf16[2,4,96,384]{3,2,1,0:T(8,128)(2,1)S(1)} %pad_maximum_fusion.30), channel_id=1, source_target_pairs={{0,4},{4,0},{1,5},{5,1},{2,6},{6,2},{3,7},{7,3},{8,12},{12,8},{9,1... | collective-permute-start | bytes 1769480 | tf_op jit(solution)/shard_map/ppermute | solution.py:19
  202.3 16.3 %collective-permute-start.77 = (bf16[4,2,96,384]{3,2,0,1:T(8,128)(2,1)S(1)}, bf16[4,2,96,384]{3,2,0,1:T(8,128)(2,1)S(1)}, u32[]{:S(2)}, u32[]{:S(2)}) collective-permute-start(bf16[4,2,96,384]{3,2,0,1:T(8,128)(2,1)S(1)} %copy.159), channel_id=1, source_target_pairs={{0,2},{2,0},{1,3},{3,1},{4,6},{6,4},{5,7},{7,5},{8,10},{10,8},{9,1... | collective-permute-start | bytes 1769480 | tf_op jit(solution)/shard_map/ppermute | solution.py:19
  207.1 21.1 %collective-permute-start.72 = (bf16[2,4,96,384]{3,2,1,0:T(8,128)(2,1)S(1)}, bf16[2,4,96,384]{3,2,1,0:T(8,128)(2,1)S(1)}, u32[]{:S(2)}, u32[]{:S(2)}) collective-permute-start(bf16[2,4,96,384]{3,2,1,0:T(8,128)(2,1)S(1)} %pad_maximum_fusion.29), channel_id=1, source_target_pairs={{0,4},{4,0},{1,5},{5,1},{2,6},{6,2},{3,7},{7,3},{8,12},{12,8},{9,1... | collective-permute-start | bytes 1769480 | tf_op jit(solution)/shard_map/ppermute | solution.py:19
  208.6 22.7 %collective-permute-start.70 = (bf16[4,2,96,384]{3,2,0,1:T(8,128)(2,1)S(1)}, bf16[4,2,96,384]{3,2,0,1:T(8,128)(2,1)S(1)}, u32[]{:S(2)}, u32[]{:S(2)}) collective-permute-start(bf16[4,2,96,384]{3,2,0,1:T(8,128)(2,1)S(1)} %copy.154), channel_id=1, source_target_pairs={{0,2},{2,0},{1,3},{3,1},{4,6},{6,4},{5,7},{7,5},{8,10},{10,8},{9,1... | collective-permute-start | bytes 1769480 | tf_op jit(solution)/shard_map/ppermute | solution.py:19
  211.2 22.1 %collective-permute-start.39 = (bf16[512,768]{1,0:T(8,128)(2,1)S(1)}, bf16[512,768]{1,0:T(8,128)(2,1)S(1)}, u32[]{:S(2)}, u32[]{:S(2)}) collective-permute-start(bf16[512,768]{1,0:T(8,128)(2,1)S(1)} %slice.1264), channel_id=1, source_target_pairs={{0,1},{1,0},{2,3},{3,2},{4,5},{5,4},{6,7},{7,6},{8,9},{9,8},{10,11... | collective-permute-start | bytes 2359304 | tf_op jit(solution)/shard_map/ppermute | solution.py:19
  217.8 16.8 %collective-permute-start.41 = (bf16[512,768]{1,0:T(8,128)(2,1)S(1)}, bf16[512,768]{1,0:T(8,128)(2,1)S(1)}, u32[]{:S(2)}, u32[]{:S(2)}) collective-permute-start(bf16[512,768]{1,0:T(8,128)(2,1)S(1)} %slice.1263), channel_id=1, source_target_pairs={{0,1},{1,0},{2,3},{3,2},{4,5},{5,4},{6,7},{7,6},{8,9},{9,8},{10,11... | collective-permute-start | bytes 2359304 | tf_op jit(solution)/shard_map/ppermute | solution.py:19
  218.7 21.3 %collective-permute-start.80 = (bf16[4,96,384]{2,1,0:T(8,128)(2,1)S(1)}, bf16[4,96,384]{2,1,0:T(8,128)(2,1)S(1)}, u32[]{:S(2)}, u32[]{:S(2)}) collective-permute-start(bf16[4,96,384]{2,1,0:T(8,128)(2,1)S(1)} %fusion.37), channel_id=1, source_target_pairs={{0,2},{2,0},{1,3},{3,1},{4,6},{6,4},{5,7},{7,5},{8,10},{10,8},{9,1... | collective-permute-start | bytes 884744 | tf_op jit(solution)/shard_map/ppermute | solution.py:19
  228.3 11.8 %collective-permute-start.78 = (bf16[4,96,384]{2,1,0:T(8,128)(2,1)S(1)}, bf16[4,96,384]{2,1,0:T(8,128)(2,1)S(1)}, u32[]{:S(2)}, u32[]{:S(2)}) collective-permute-start(bf16[4,96,384]{2,1,0:T(8,128)(2,1)S(1)} %fusion.63), channel_id=1, source_target_pairs={{0,4},{4,0},{1,5},{5,1},{2,6},{6,2},{3,7},{7,3},{8,12},{12,8},{9,1... | collective-permute-start | bytes 884744 | tf_op jit(solution)/shard_map/ppermute | solution.py:19
  231.3 11.7 %collective-permute-start.73 = (bf16[4,96,384]{2,1,0:T(8,128)(2,1)S(1)}, bf16[4,96,384]{2,1,0:T(8,128)(2,1)S(1)}, u32[]{:S(2)}, u32[]{:S(2)}) collective-permute-start(bf16[4,96,384]{2,1,0:T(8,128)(2,1)S(1)} %fusion.39), channel_id=1, source_target_pairs={{0,2},{2,0},{1,3},{3,1},{4,6},{6,4},{5,7},{7,5},{8,10},{10,8},{9,1... | collective-permute-start | bytes 884744 | tf_op jit(solution)/shard_map/ppermute | solution.py:19
  233.2 11.7 %collective-permute-start.71 = (bf16[4,96,384]{2,1,0:T(8,128)(2,1)S(1)}, bf16[4,96,384]{2,1,0:T(8,128)(2,1)S(1)}, u32[]{:S(2)}, u32[]{:S(2)}) collective-permute-start(bf16[4,96,384]{2,1,0:T(8,128)(2,1)S(1)} %fusion.62), channel_id=1, source_target_pairs={{0,4},{4,0},{1,5},{5,1},{2,6},{6,2},{3,7},{7,3},{8,12},{12,8},{9,1... | collective-permute-start | bytes 884744 | tf_op jit(solution)/shard_map/ppermute | solution.py:19
  240.0 27.9 %collective-permute-start.42 = (bf16[512,768]{1,0:T(8,128)(2,1)S(1)}, bf16[512,768]{1,0:T(8,128)(2,1)S(1)}, u32[]{:S(2)}, u32[]{:S(2)}) collective-permute-start(bf16[512,768]{1,0:T(8,128)(2,1)S(1)} %get-tuple-element.76), channel_id=1, source_target_pairs={{0,1},{1,0},{2,3},{3,2},{4,5},{5,4},{6,7},{7,6},{8,9},{9,8},{10,11... | collective-permute-start | bytes 2359304 | tf_op jit(solution)/shard_map/ppermute | solution.py:19
  240.4 14.0 %collective-permute-start.82 = (bf16[96,768]{1,0:T(8,128)(2,1)S(1)}, bf16[96,768]{1,0:T(8,128)(2,1)S(1)}, u32[]{:S(2)}, u32[]{:S(2)}) collective-permute-start(bf16[96,768]{1,0:T(8,128)(2,1)S(1)} %get-tuple-element.100), channel_id=1, source_target_pairs={{0,16},{8,24},{16,0},{24,8},{1,17},{9,25},{17,1},{25,9},{2,18},{10... | collective-permute-start | bytes 442376 | tf_op jit(solution)/shard_map/ppermute | solution.py:40
  243.0 13.5 %collective-permute-start.83 = (bf16[96,768]{1,0:T(8,128)(2,1)S(1)}, bf16[96,768]{1,0:T(8,128)(2,1)S(1)}, u32[]{:S(2)}, u32[]{:S(2)}) collective-permute-start(bf16[96,768]{1,0:T(8,128)(2,1)S(1)} %get-tuple-element.99), channel_id=1, source_target_pairs={{0,24},{8,16},{16,8},{24,0},{1,25},{9,17},{17,9},{25,1},{2,26},{10... | collective-permute-start | bytes 442376 | tf_op jit(solution)/shard_map/ppermute | solution.py:40
  245.3 11.9 %collective-permute-start.74 = (bf16[96,768]{1,0:T(8,128)(2,1)S(1)}, bf16[96,768]{1,0:T(8,128)(2,1)S(1)}, u32[]{:S(2)}, u32[]{:S(2)}) collective-permute-start(bf16[96,768]{1,0:T(8,128)(2,1)S(1)} %get-tuple-element.101), channel_id=1, source_target_pairs={{0,8},{8,0},{16,24},{24,16},{1,9},{9,1},{17,25},{25,17},{2,10},{10... | collective-permute-start | bytes 442376 | tf_op jit(solution)/shard_map/ppermute | solution.py:40
  249.5 17.5 %collective-permute-start.75 = (bf16[96,768]{1,0:T(8,128)(2,1)S(1)}, bf16[96,768]{1,0:T(8,128)(2,1)S(1)}, u32[]{:S(2)}, u32[]{:S(2)}) collective-permute-start(bf16[96,768]{1,0:T(8,128)(2,1)S(1)} %get-tuple-element.103), channel_id=1, source_target_pairs={{0,16},{8,24},{16,0},{24,8},{1,17},{9,25},{17,1},{25,9},{2,18},{10... | collective-permute-start | bytes 442376 | tf_op jit(solution)/shard_map/ppermute | solution.py:40
  254.4 12.6 %collective-permute-start.76 = (bf16[96,768]{1,0:T(8,128)(2,1)S(1)}, bf16[96,768]{1,0:T(8,128)(2,1)S(1)}, u32[]{:S(2)}, u32[]{:S(2)}) collective-permute-start(bf16[96,768]{1,0:T(8,128)(2,1)S(1)} %get-tuple-element.102), channel_id=1, source_target_pairs={{0,24},{8,16},{16,8},{24,0},{1,25},{9,17},{17,9},{25,1},{2,26},{10... | collective-permute-start | bytes 442376 | tf_op jit(solution)/shard_map/ppermute | solution.py:40
  351.7 40.8 %collective-permute-start.51 = (bf16[2,4,96,128]{3,2,1,0:T(8,128)(2,1)}, bf16[2,4,96,128]{3,2,1,0:T(8,128)(2,1)}, u32[]{:S(2)}, u32[]{:S(2)}) collective-permute-start(bf16[2,4,96,128]{3,2,1,0:T(8,128)(2,1)} %pad_maximum_fusion.68), channel_id=1, source_target_pairs={{0,4},{4,0},{1,5},{5,1},{2,6},{6,2},{3,7},{7,3},{8,12},{12,8},{9,1... | collective-permute-start | bytes 589832 | tf_op jit(solution)/shard_map/ppermute | solution.py:19
  354.1 37.1 %collective-permute-start.49 = (bf16[4,2,96,128]{3,2,0,1:T(8,128)(2,1)}, bf16[4,2,96,128]{3,2,0,1:T(8,128)(2,1)}, u32[]{:S(2)}, u32[]{:S(2)}) collective-permute-start(bf16[4,2,96,128]{3,2,0,1:T(8,128)(2,1)} %copy.138), channel_id=1, source_target_pairs={{0,2},{2,0},{1,3},{3,1},{4,6},{6,4},{5,7},{7,5},{8,10},{10,8},{9,1... | collective-permute-start | bytes 589832 | tf_op jit(solution)/shard_map/ppermute | solution.py:19
  365.4 31.0 %collective-permute-start.58 = (bf16[2,4,96,128]{3,2,1,0:T(8,128)(2,1)}, bf16[2,4,96,128]{3,2,1,0:T(8,128)(2,1)}, u32[]{:S(2)}, u32[]{:S(2)}) collective-permute-start(bf16[2,4,96,128]{3,2,1,0:T(8,128)(2,1)} %pad_maximum_fusion.69), channel_id=1, source_target_pairs={{0,4},{4,0},{1,5},{5,1},{2,6},{6,2},{3,7},{7,3},{8,12},{12,8},{9,1... | collective-permute-start | bytes 589832 | tf_op jit(solution)/shard_map/ppermute | solution.py:19
  367.4 26.2 %collective-permute-start.56 = (bf16[4,2,96,128]{3,2,0,1:T(8,128)(2,1)}, bf16[4,2,96,128]{3,2,0,1:T(8,128)(2,1)}, u32[]{:S(2)}, u32[]{:S(2)}) collective-permute-start(bf16[4,2,96,128]{3,2,0,1:T(8,128)(2,1)} %copy.142), channel_id=1, source_target_pairs={{0,2},{2,0},{1,3},{3,1},{4,6},{6,4},{5,7},{7,5},{8,10},{10,8},{9,1... | collective-permute-start | bytes 589832 | tf_op jit(solution)/shard_map/ppermute | solution.py:19
  379.6 19.6 %collective-permute-start.65 = (bf16[2,4,96,128]{3,2,1,0:T(8,128)(2,1)S(1)}, bf16[2,4,96,128]{3,2,1,0:T(8,128)(2,1)S(1)}, u32[]{:S(2)}, u32[]{:S(2)}) collective-permute-start(bf16[2,4,96,128]{3,2,1,0:T(8,128)(2,1)S(1)} %pad_maximum_fusion.70), channel_id=1, source_target_pairs={{0,4},{4,0},{1,5},{5,1},{2,6},{6,2},{3,7},{7,3},{8,12},{12,8},{9,1... | collective-permute-start | bytes 589832 | tf_op jit(solution)/shard_map/ppermute | solution.py:19
  392.5 33.3 %collective-permute-start.43 = (bf16[512,768]{1,0:T(8,128)(2,1)S(1)}, bf16[512,768]{1,0:T(8,128)(2,1)S(1)}, u32[]{:S(2)}, u32[]{:S(2)}) collective-permute-start(bf16[512,768]{1,0:T(8,128)(2,1)S(1)} %slice.1262), channel_id=1, source_target_pairs={{0,1},{1,0},{2,3},{3,2},{4,5},{5,4},{6,7},{7,6},{8,9},{9,8},{10,11... | collective-permute-start | bytes 2359304 | tf_op jit(solution)/shard_map/ppermute | solution.py:19
  399.1 9.6 %collective-permute-start.57 = (bf16[4,96,128]{2,1,0:T(8,128)(2,1)S(1)}, bf16[4,96,128]{2,1,0:T(8,128)(2,1)S(1)}, u32[]{:S(2)}, u32[]{:S(2)}) collective-permute-start(bf16[4,96,128]{2,1,0:T(8,128)(2,1)S(1)} %fusion.84), channel_id=1, source_target_pairs={{0,4},{4,0},{1,5},{5,1},{2,6},{6,2},{3,7},{7,3},{8,12},{12,8},{9,1... | collective-permute-start | bytes 294920 | tf_op jit(solution)/shard_map/ppermute | solution.py:19
  400.0 9.4 %collective-permute-start.66 = (bf16[4,96,128]{2,1,0:T(8,128)(2,1)S(1)}, bf16[4,96,128]{2,1,0:T(8,128)(2,1)S(1)}, u32[]{:S(2)}, u32[]{:S(2)}) collective-permute-start(bf16[4,96,128]{2,1,0:T(8,128)(2,1)S(1)} %fusion.75), channel_id=1, source_target_pairs={{0,2},{2,0},{1,3},{3,1},{4,6},{6,4},{5,7},{7,5},{8,10},{10,8},{9,1... | collective-permute-start | bytes 294920 | tf_op jit(solution)/shard_map/ppermute | solution.py:19
  (125 other events, 779.0 us)

commit v2 on v1

v2 whole, which is shorter than its diff:
```python
import math
from functools import partial

import jax
import jax.numpy as jnp
from jax import lax
from jax.experimental import pallas as pl
from jax.experimental.pallas import tpu as pltpu
from jax.sharding import Mesh, PartitionSpec as P

HEAD_DIM = 64
EPSILON = 1e-06
SWAP = [(0, 1), (1, 0)]
LOG2E = math.log2(math.e)
BF16 = jnp.bfloat16
F32 = jnp.float32


def swap(array, axis):
    return lax.ppermute(array, axis, SWAP)


def dot_nn(left, right):
    return lax.dot_general(left, right, (((1,), (0,)), ((), ())), preferred_element_type=F32)


def dot_nt(left, right):
    return lax.dot_general(left, right, (((1,), (1,)), ((), ())), preferred_element_type=F32)


def dot_tn(left, right):
    return lax.dot_general(left, right, (((0,), (0,)), ((), ())), preferred_element_type=F32)


def xor_exchange(blocks_of, axes):
    got = {}
    count = len(axes)
    sizes = [2] * count
    for bits in range(1, 2**count):
        perm = [(i, i ^ bits) for i in range(math.prod(sizes))]
        got[bits] = lax.ppermute(blocks_of(bits), axes, perm)
    return got


def in_order(own, got, axes):
    parts = [own] + [got[bits] for bits in range(1, 2 ** len(axes))]
    for depth, axis in enumerate(reversed(axes)):
        bit = 2**depth
        flip = lax.axis_index(axis) == 1
        parts = [jnp.where(flip, parts[i ^ bit], parts[i]) for i in range(len(parts))]
    return jnp.stack(parts)


def pair_in_order(own, other, axis, dim):
    flip = lax.axis_index(axis) == 1
    return jnp.stack([jnp.where(flip, other, own), jnp.where(flip, own, other)], axis=dim)


def gather_rows(shard, rows):
    low, high = rows[-1], rows[:-1]
    n, c = shard.shape
    near = high[-2:]
    stack = in_order(shard, xor_exchange(lambda bits: shard, near), near)
    for axis in reversed(high[:-2]):
        other = swap(stack, axis)
        stack = pair_in_order(stack, other, axis, 0).reshape(-1, n, c)
    half = c // 2
    first, second = stack[:, :, :half], stack[:, :, half:]
    first_low, second_y = swap(first, low), swap(second, "y")
    first = pair_in_order(first, first_low, low, 1).reshape(-1, half)
    first_y = swap(first, "y")
    second_low = swap(jnp.stack([second, second_y]), low)
    second_own = pair_in_order(second, second_low[0], low, 1).reshape(-1, half)
    second_other = pair_in_order(second_y, second_low[1], low, 1).reshape(-1, half)
    return (
        jnp.concatenate([first, second_own], axis=1),
        jnp.concatenate([first_y, second_other], axis=1),
    )


def pick(array, axis, dim, other):
    zero = lax.index_in_dim(array, 0, dim, keepdims=False)
    one = lax.index_in_dim(array, 1, dim, keepdims=False)
    flip = lax.axis_index(axis) == (0 if other else 1)
    return jnp.where(flip, one, zero)


def scatter_rows(own, other, rows):
    low, high = rows[-1], rows[:-1]
    near = high[-2:]
    total = 2 ** len(rows)
    n, c = own.shape[0] // total, own.shape[1]
    half = c // 2
    own = own.reshape(total // 2, 2, n, c)
    other = other.reshape(total // 2, 2, n, c)
    a_own, a_other = own[..., :half], other[..., :half]
    b_own, b_other = own[..., half:], other[..., half:]
    a_got = swap(a_other, "y")
    b_send = jnp.stack([pick(b_own, low, 1, True), pick(b_other, low, 1, True)])
    b_got = swap(b_send, low)
    a_sum = a_own.astype(F32) + a_got.astype(F32)
    a_send = pick(a_sum, low, 1, True).astype(BF16)
    b_own = pick(b_own, low, 1, False).astype(F32) + b_got[0].astype(F32)
    b_other = (pick(b_other, low, 1, False).astype(F32) + b_got[1].astype(F32)).astype(BF16)
    a_got = swap(a_send, low)
    b_got = swap(b_other, "y")
    a_sum = pick(a_sum, low, 1, False) + a_got.astype(F32)
    b_sum = b_own + b_got.astype(F32)
    both = jnp.concatenate([a_sum, b_sum], axis=2)
    for axis in high[:-2]:
        both = both.reshape(2, -1, n, c)
        got = swap(pick(both, axis, 0, True).astype(BF16), axis)
        both = pick(both, axis, 0, False) + got.astype(F32)
    low_both = both.astype(BF16)
    place = lax.axis_index(near)
    take = lambda bits: lax.dynamic_index_in_dim(low_both, place ^ bits, 0, keepdims=False)
    got = xor_exchange(take, near)
    out = lax.dynamic_index_in_dim(both, place, 0, keepdims=False)
    for piece in got.values():
        out = out + piece.astype(F32)
    return out


def gather_near(shard, near):
    got = xor_exchange(lambda bits: shard, near)
    return jnp.stack([shard] + [got[bits] for bits in range(1, 2 ** len(near))])


def gather_far(stack, low):
    half = stack.shape[0] // 2
    from_low = swap(stack, low)
    from_y = swap(stack, "y")
    corner_a = swap(from_low[:half], "y")
    corner_b = swap(from_y[half:], low)
    return stack, from_low, from_y, corner_a, corner_b


def assemble_kernel(rows, xor, s_ref, x_ref, y_ref, a_ref, b_ref, out_ref, sems):
    count, n, c = s_ref.shape
    x = lax.axis_index(rows[-1])
    z = lax.axis_index(rows[:-1])
    half = count // 2
    copies = []
    for k in range(count):
        corner = a_ref.at[k] if k < half else b_ref.at[k - half]
        at = lax.bitwise_xor(z, k) if xor else k
        sources = ((s_ref.at[k], 0, 0), (x_ref.at[k], 1, 0), (y_ref.at[k], 0, 1), (corner, 1, 1))
        for source, flip, side in sources:
            row = pl.multiple_of((at * 2 + lax.bitwise_xor(x, flip)) * n, n)
            target = out_ref.at[pl.ds(row, n), pl.ds(side * c, c)]
            copies.append(pltpu.make_async_copy(source, target, sems.at[len(copies)]))
    for copy in copies:
        copy.start()
    for copy in copies:
        copy.wait()


def assemble(pieces, rows, xor):
    count, n, c = pieces[0].shape
    anywhere = pl.BlockSpec(memory_space=pl.ANY)
    return pl.pallas_call(
        partial(assemble_kernel, rows, xor),
        in_specs=[anywhere] * 5,
        out_specs=anywhere,
        out_shape=jax.ShapeDtypeStruct((count * 2 * n, 2 * c), BF16),
        scratch_shapes=[pltpu.SemaphoreType.DMA((4 * count,))],
        cost_estimate=pl.CostEstimate(
            flops=0, bytes_accessed=16 * count * n * c * 2, transcendentals=0
        ),
        name="assemble",
    )(*pieces)


def reduce_far(parts, low):
    own, to_low, to_y, corner_a, corner_b = parts
    half = own.shape[0] // 2
    got_a = swap(corner_a, "y")
    got_b = swap(corner_b, low)
    add = lambda a, b: (a.astype(F32) + b.astype(F32)).astype(BF16)
    to_low = jnp.concatenate([add(to_low[:half], got_a), to_low[half:]])
    to_y = jnp.concatenate([to_y[:half], add(to_y[half:], got_b)])
    got_low = swap(to_low, low)
    got_y = swap(to_y, "y")
    total = own.astype(F32) + got_low.astype(F32) + got_y.astype(F32)
    return total.astype(BF16)


def reduce_near(stack, near):
    n, c = stack.shape[1:]
    return lax.psum_scatter(stack.reshape(-1, c), near, scatter_dimension=0, tiled=True)


def turn(rows, n, left_refs, turned_ref):
    at = 0
    for ref in left_refs:
        tokens = ref.shape[0]
        turned = ref[...].T
        if rows is None:
            turned_ref[:, at : at + tokens] = turned
            at += tokens
            continue
        count = turned.shape[0] // n // 2
        for block in range(2 * count):
            z, x = divmod(block, 2)
            slot = lax.bitwise_xor(lax.axis_index(rows[-1]), x) * count + z
            turned_ref[pl.ds(pl.multiple_of(slot * n, n), n), at : at + tokens] = turned[
                block * n : (block + 1) * n, :
            ]
        at += tokens


def store_grads(own, other, refs, cols):
    s_ref, x_ref, y_ref, a_ref, b_ref = refs
    half = own.shape[0] // 2
    quarter = half // 2
    s_ref[:, cols] = own[:half].astype(BF16)
    x_ref[:, cols] = own[half:].astype(BF16)
    y_ref[:, cols] = other[:half].astype(BF16)
    a_ref[:, cols] = other[half : half + quarter].astype(BF16)
    b_ref[:, cols] = other[half + quarter :].astype(BF16)


def grad_shapes(width, c):
    return [
        jax.ShapeDtypeStruct((width // 2, c), BF16),
        jax.ShapeDtypeStruct((width // 2, c), BF16),
        jax.ShapeDtypeStruct((width // 2, c), BF16),
        jax.ShapeDtypeStruct((width // 4, c), BF16),
        jax.ShapeDtypeStruct((width // 4, c), BF16),
    ]


def whole(shape):
    return pl.BlockSpec(shape, lambda *_: (0,) * len(shape))


def attend_forward_kernel(
    xa_ref, xb_ref, w_ref, bias_ref, q_ref, k_ref, v_ref, mixed_ref, lse_ref, wcat_ref, vt_ref
):
    pair, step = pl.program_id(0), pl.program_id(1)
    block = mixed_ref.shape[0]
    d = HEAD_DIM
    pairs = q_ref.shape[0]
    side = pairs * d

    @pl.when((pair == 0) & (step == 0))
    def _():
        tokens = xa_ref.shape[0]
        for kind in range(4):
            weight = jnp.concatenate(
                [
                    w_ref[:, kind * side : (kind + 1) * side],
                    w_ref[:, (4 + kind) * side : (5 + kind) * side],
                ],
                axis=1,
            )
            wcat_ref[:, kind * 2 * side : (kind + 1) * 2 * side] = weight
            if kind == 3:
                break
            target = (q_ref, k_ref, v_ref)[kind]
            for half, ref in enumerate((xa_ref, xb_ref)):
                proj = (dot_nn(ref[...], weight) + bias_ref[kind : kind + 1, :]).astype(BF16)
                for p in range(pairs):
                    target[p, half * tokens : (half + 1) * tokens, :] = proj[
                        :, p * 2 * d : (p + 1) * 2 * d
                    ]

    @pl.when(step == 0)
    def _():
        vt = v_ref[pair].T
        for head in range(2):
            vt_ref[head, :d, :] = vt[head * d : (head + 1) * d, :]
            vt_ref[head, d:, :] = jnp.ones((vt_ref.shape[1] - d, vt.shape[1]), BF16)

    query = q_ref[pair, pl.ds(pl.multiple_of(step * block, block), block), :]
    lane = lax.broadcasted_iota(jnp.int32, query.shape, 1)
    outs = []
    for head in range(2):
        masked = jnp.where(lane // d == head, query, jnp.zeros_like(query)) * BF16(d**-0.5)
        scores = dot_nt(k_ref[pair], masked)
        top = jnp.max(scores, axis=0, keepdims=True)
        weights = jnp.exp2((scores - top) * LOG2E).astype(BF16)
        out = dot_nn(vt_ref[head], weights)
        total = out[d : d + 1, :]
        outs.append(out[:d, :] * (1.0 / total))
        lse_ref[0, head : head + 1, :] = top + jnp.log(total)
    mixed_ref[...] = jnp.concatenate(outs, axis=0).T.astype(BF16)


def attend_forward(xa, xb, weight, bias):
    seq = xa.shape[0] * 2
    width = xa.shape[1]
    block = 256
    two = 2 * HEAD_DIM
    pairs = weight.shape[1] // (4 * two)
    out = jax.ShapeDtypeStruct((pairs, seq, two), BF16)
    return pl.pallas_call(
        attend_forward_kernel,
        grid=(pairs, seq // block),
        in_specs=[whole(xa.shape), whole(xb.shape), whole(weight.shape), whole(bias.shape)],
        out_specs=[
            whole(out.shape),
            whole(out.shape),
            whole(out.shape),
            pl.BlockSpec((block, two), lambda p, i: (i, p)),
            pl.BlockSpec((1, 8, block), lambda p, i: (p, 0, i)),
            whole(weight.shape),
        ],
        out_shape=[
            out,
            out,
            out,
            jax.ShapeDtypeStruct((seq, pairs * two), BF16),
            jax.ShapeDtypeStruct((pairs, 8, seq), F32),
            jax.ShapeDtypeStruct(weight.shape, BF16),
        ],
        scratch_shapes=[pltpu.VMEM((2, HEAD_DIM + 16, seq), BF16)],
        cost_estimate=pl.CostEstimate(
            flops=pairs * 24 * seq * seq * two,
            bytes_accessed=16 * seq * width,
            transcendentals=pairs * 2 * seq * seq,
        ),
        name="attend_forward",
    )(xa, xb, weight, bias)


def attend_backward_kernel(
    q_ref, k_ref, v_ref, grad_ref, mixed_ref, lse_ref, dproj_ref, kt_ref, dk_acc, dv_acc
):
    pair, step = pl.program_id(0), pl.program_id(1)
    block = q_ref.shape[1]
    d = HEAD_DIM
    two = 2 * d
    scale = d**-0.5
    span = dproj_ref.shape[1] // 3

    @pl.when(step == 0)
    def _():
        kt_ref[...] = k_ref[0].T
        dk_acc[...] = jnp.zeros_like(dk_acc)
        dv_acc[...] = jnp.zeros_like(dv_acc)

    query = q_ref[0]
    grad = grad_ref[...]
    lane = lax.broadcasted_iota(jnp.int32, query.shape, 1)
    dots = (grad.astype(F32) * mixed_ref[...].astype(F32)).T
    dqs = []
    for head in range(2):
        mine = lane // d == head
        query_h = jnp.where(mine, query, jnp.zeros_like(query))
        grad_h = jnp.where(mine, grad, jnp.zeros_like(grad))
        row_dots = jnp.sum(dots[head * d : (head + 1) * d, :], axis=0, keepdims=True)
        log_total = lse_ref[0, head : head + 1, :] * LOG2E
        scores = dot_nt(k_ref[0], query_h * BF16(scale))
        probs = jnp.exp2(scores * LOG2E - log_total)
        grad_probs = dot_nt(v_ref[0], grad_h)
        grad_scores = (probs * (grad_probs - row_dots)).astype(BF16)
        dv_acc[...] += dot_nn(probs.astype(BF16), grad_h)
        dk_acc[...] += dot_nn(grad_scores, query_h)
        dqs.append(dot_nn(kt_ref[head * d : (head + 1) * d, :], grad_scores) * scale)
    rows = pl.ds(pl.multiple_of(step * block, block), block)
    col = pl.multiple_of(pair * two, two)
    dproj_ref[rows, pl.ds(col, two)] = jnp.concatenate(dqs, axis=0).T.astype(BF16)

    @pl.when(step == pl.num_programs(1) - 1)
    def _():
        dproj_ref[:, pl.ds(span + col, two)] = (dk_acc[...] * scale).astype(BF16)
        dproj_ref[:, pl.ds(2 * span + col, two)] = dv_acc[...].astype(BF16)


def attend_backward(q, k, v, grad, mixed, lse):
    pairs, seq, two = q.shape
    block = 256
    full = pl.BlockSpec((1, seq, two), lambda p, i: (p, 0, 0))
    part = pl.BlockSpec((block, two), lambda p, i: (i, p))
    return pl.pallas_call(
        attend_backward_kernel,
        grid=(pairs, seq // block),
        in_specs=[
            pl.BlockSpec((1, block, two), lambda p, i: (p, i, 0)),
            full,
            full,
            part,
            part,
            pl.BlockSpec((1, 8, block), lambda p, i: (p, 0, i)),
        ],
        out_specs=whole((seq, 3 * pairs * two)),
        out_shape=jax.ShapeDtypeStruct((seq, 3 * pairs * two), BF16),
        scratch_shapes=[
            pltpu.VMEM((two, seq), BF16),
            pltpu.VMEM((seq, two), F32),
            pltpu.VMEM((seq, two), F32),
        ],
        cost_estimate=pl.CostEstimate(
            flops=pairs * 50 * seq * seq * two,
            bytes_accessed=pairs * 20 * seq * two,
            transcendentals=pairs * 2 * seq * seq,
        ),
        name="attend_backward",
    )(q, k, v, grad, mixed, lse)


def attention_grads_kernel(
    rows, n, xa_ref, xb_ref, ga_ref, gb_ref, dproj_ref, mixed_ref, s_ref, x_ref, y_ref, a_ref, b_ref,
    turned_ref,
):
    refs = (s_ref, x_ref, y_ref, a_ref, b_ref)
    side = mixed_ref.shape[1] // 2
    turn(rows, n, (xa_ref, xb_ref), turned_ref)
    for kind in range(3):
        both = dproj_ref[:, kind * 2 * side : (kind + 1) * 2 * side]
        grads = dot_nn(turned_ref[...], both)
        store_grads(
            grads[:, :side], grads[:, side:], refs, slice(kind * side, (kind + 1) * side)
        )
    turn(rows, n, (ga_ref, gb_ref), turned_ref)
    grads = dot_nn(turned_ref[...], mixed_ref[...])
    store_grads(grads[:, :side], grads[:, side:], refs, slice(3 * side, 4 * side))


def attention_grads(xa, xb, ga, gb, dproj, mixed, rows, n):
    tokens, width = xa.shape
    c = 2 * mixed.shape[1]
    return pl.pallas_call(
        partial(attention_grads_kernel, rows, n),
        out_shape=grad_shapes(width, c),
        scratch_shapes=[pltpu.VMEM((width, 2 * tokens), BF16)],
        cost_estimate=pl.CostEstimate(
            flops=4 * tokens * width * 2 * c, bytes_accessed=8 * width * c, transcendentals=0
        ),
        name="attention_grads",
    )(xa, xb, ga, gb, dproj, mixed)


def gelu_parts(u):
    c0 = math.sqrt(2.0 / math.pi)
    square = u * u
    t = jnp.tanh(u * (c0 + (c0 * 0.044715) * square))
    half = 0.5 * u
    act = half + half * t
    slope = 0.5 + 0.5 * t + half * (1.0 - t * t) * (c0 + (3.0 * c0 * 0.044715) * square)
    return act, slope


def up_kernel(
    rows, n, xa_ref, xb_ref, ga_ref, gb_ref, w_ref, wo_ref, bias_ref, bias_o_ref,
    act_ref, slope_ref, act_o_ref, slope_o_ref, s_ref, x_ref, y_ref, a_ref, b_ref, turned_ref,
):
    @pl.when(pl.program_id(0) == 0)
    def _():
        turn(rows, n, (ga_ref, gb_ref), turned_ref)

    tokens = xa_ref.shape[0]
    grads = []
    for weight, bias, acts, slopes in (
        (w_ref, bias_ref, act_ref, slope_ref),
        (wo_ref, bias_o_ref, act_o_ref, slope_o_ref),
    ):
        for half, ref in enumerate((xa_ref, xb_ref)):
            act, slope = gelu_parts(dot_nn(ref[...], weight[...]) + bias[0:1, :])
            acts[half * tokens : (half + 1) * tokens, :] = act.astype(BF16)
            slopes[half * tokens : (half + 1) * tokens, :] = slope.astype(BF16)
        grads.append(dot_nn(turned_ref[...], acts[...]))
    store_grads(*grads, (s_ref, x_ref, y_ref, a_ref, b_ref), slice(None))


def up_and_down_grads(xa, xb, ga, gb, weight, bias, bias_o, rows, n):
    tokens, width = xa.shape
    c = weight.shape[1] // 2
    tile = 256
    steps = c // tile
    hidden = jax.ShapeDtypeStruct((2 * tokens, c), BF16)
    cols = lambda r: pl.BlockSpec((r, tile), lambda j: (0, j))
    return pl.pallas_call(
        partial(up_kernel, rows, n),
        grid=(steps,),
        in_specs=[whole(xa.shape)] * 4
        + [
            cols(width),
            pl.BlockSpec((width, tile), lambda j: (0, j + steps)),
            cols(8),
            cols(8),
        ],
        out_specs=[cols(2 * tokens)] * 4 + [cols(s.shape[0]) for s in grad_shapes(width, c)],
        out_shape=[hidden] * 4 + grad_shapes(width, c),
        scratch_shapes=[pltpu.VMEM((width, 2 * tokens), BF16)],
        cost_estimate=pl.CostEstimate(
            flops=16 * tokens * width * c,
            bytes_accessed=24 * tokens * c,
            transcendentals=4 * tokens * c,
        ),
        name="up_and_down_grads",
    )(xa, xb, ga, gb, weight, weight, bias, bias_o)


def hidden_back_kernel(
    ga_ref, gb_ref, w_ref, wo_ref, u_ref, uo_ref, slope_ref, slope_o_ref,
    pre_ref, pre_o_ref, sum_ref, own_ref, other_ref, acc_ref,
):
    step = pl.program_id(0)
    tokens = ga_ref.shape[0]

    @pl.when(step == 0)
    def _():
        acc_ref[...] = jnp.zeros_like(acc_ref)

    for side, (weight, up, slopes, pres) in enumerate(
        ((w_ref, u_ref, slope_ref, pre_ref), (wo_ref, uo_ref, slope_o_ref, pre_o_ref))
    ):
        totals = 0.0
        for half, ref in enumerate((ga_ref, gb_ref)):
            at = slice(half * tokens, (half + 1) * tokens)
            back = dot_nn(ref[...], weight[...]) * slopes[at, :].astype(F32)
            pre = back.astype(BF16)
            pres[at, :] = pre
            totals = totals + jnp.sum(pre.astype(F32), axis=0, keepdims=True)
            acc_ref[at, :] += dot_nt(pre, up[...])
        sum_ref[side : side + 1, :] = totals

    @pl.when(step == pl.num_programs(0) - 1)
    def _():
        own_ref[...] = acc_ref[:tokens, :]
        other_ref[...] = acc_ref[tokens:, :].astype(BF16)


def hidden_back(ga, gb, down, up, slope, slope_o):
    tokens, width = ga.shape
    c = down.shape[1] // 2
    tile = 256
    steps = c // tile
    cols = lambda r: pl.BlockSpec((r, tile), lambda j: (0, j))
    far = lambda r: pl.BlockSpec((r, tile), lambda j: (0, j + steps))
    hidden = jax.ShapeDtypeStruct((2 * tokens, c), BF16)
    return pl.pallas_call(
        hidden_back_kernel,
        grid=(steps,),
        in_specs=[
            whole(ga.shape),
            whole(ga.shape),
            cols(width),
            far(width),
            cols(width),
            far(width),
            cols(2 * tokens),
            cols(2 * tokens),
        ],
        out_specs=[
            cols(2 * tokens),
            cols(2 * tokens),
            cols(8),
            whole(ga.shape),
            whole(ga.shape),
        ],
        out_shape=[
            hidden,
            hidden,
            jax.ShapeDtypeStruct((8, c), F32),
            jax.ShapeDtypeStruct(ga.shape, F32),
            jax.ShapeDtypeStruct(ga.shape, BF16),
        ],
        scratch_shapes=[pltpu.VMEM((2 * tokens, width), F32)],
        cost_estimate=pl.CostEstimate(
            flops=16 * tokens * width * c, bytes_accessed=24 * tokens * c, transcendentals=0
        ),
        name="hidden_back",
    )(ga, gb, down, down, up, up, slope, slope_o)


def weight_grads_kernel(
    rows, n, xa_ref, xb_ref, g_ref, go_ref, s_ref, x_ref, y_ref, a_ref, b_ref, turned_ref
):
    @pl.when(pl.program_id(0) == 0)
    def _():
        turn(rows, n, (xa_ref, xb_ref), turned_ref)

    own = dot_nn(turned_ref[...], g_ref[...])
    other = dot_nn(turned_ref[...], go_ref[...])
    store_grads(own, other, (s_ref, x_ref, y_ref, a_ref, b_ref), slice(None))


def weight_grads(xa, xb, grad, grad_o, rows, n):
    tokens, width = xa.shape
    c = grad.shape[1]
    tile = 256
    cols = lambda r: pl.BlockSpec((r, tile), lambda j: (0, j))
    return pl.pallas_call(
        partial(weight_grads_kernel, rows, n),
        grid=(c // tile,),
        in_specs=[whole(xa.shape), whole(xa.shape), cols(2 * tokens), cols(2 * tokens)],
        out_specs=[cols(s.shape[0]) for s in grad_shapes(width, c)],
        out_shape=grad_shapes(width, c),
        scratch_shapes=[pltpu.VMEM((width, 2 * tokens), BF16)],
        cost_estimate=pl.CostEstimate(
            flops=8 * tokens * width * c, bytes_accessed=12 * tokens * c, transcendentals=0
        ),
        name="weight_grads",
    )(xa, xb, grad, grad_o)


def norm(resid, gain, shift):
    mean = jnp.mean(resid, axis=1, keepdims=True)
    centered = resid - mean
    inverse = lax.rsqrt(jnp.mean(jnp.square(centered), axis=1, keepdims=True) + EPSILON)
    hat = centered * inverse
    return (hat * gain + shift).astype(BF16), hat, inverse


def norm_back(grad, hat, inverse, gain):
    gain_grad = jnp.sum(grad * hat, axis=0)
    shift_grad = jnp.sum(grad, axis=0)
    grad_hat = grad * gain
    first = jnp.mean(grad_hat, axis=1, keepdims=True)
    second = jnp.mean(grad_hat * hat, axis=1, keepdims=True)
    return inverse * (grad_hat - first - hat * second), gain_grad, shift_grad


def make_local(rows):
    low, near = rows[-1], rows[:-1]

    def local(
        layer_input,
        attn_gain,
        attn_shift,
        qkv_weight,
        qkv_bias,
        output_weight,
        output_bias,
        mlp_gain,
        mlp_shift,
        up_weight,
        up_bias,
        down_weight,
        down_bias,
        cotangent,
    ):
        tokens, width = layer_input.shape
        n, _, side = qkv_weight.shape
        hidden = up_weight.shape[1]
        fast = n % 16 == 0 and len(near) == 2
        order = rows if fast else None

        def gather(shard, xor):
            if not fast:
                return jnp.concatenate(gather_rows(shard, rows), axis=1)
            if xor:
                stack = gather_near(shard, near)
            else:
                stack = shard
            return assemble(gather_far(stack, low), rows, xor)

        def reduce(parts):
            if not fast:
                own = jnp.concatenate(parts[:2])
                other = jnp.concatenate(parts[2:])
                return scatter_rows(own, other, rows)
            shape = (-1, n, parts[0].shape[1])
            stack = reduce_far([p.reshape(shape) for p in parts], low)
            return reduce_near(stack, near).astype(F32)

        attn_shard = jnp.concatenate([qkv_weight.reshape(n, -1), output_weight], axis=1)
        bias_pack = jnp.concatenate([qkv_bias.reshape(-1), up_bias])
        bias_other = swap(bias_pack, "y")
        qkv_bias_other = bias_other[: 2 * side].reshape(2, side)
        up_bias_other = bias_other[2 * side :]

        residual = layer_input.astype(F32)
        attn_in, attn_hat, attn_inverse = norm(residual, attn_gain, attn_shift)
        attn_in_other = swap(attn_in, "core")
        attn_full = gather(attn_shard, True)
        if fast:
            both = lax.all_gather(jnp.stack([up_weight, down_weight]), near, axis=0)
            both = both.reshape(-1, 2, n, hidden)
            up_full = gather(both[:, 0], False)
            down_full = gather(both[:, 1], False)
        else:
            up_full, down_full = gather(up_weight, True), gather(down_weight, True)
        cot_other = swap(cotangent, "core")

        both_bias = jnp.concatenate([qkv_bias, qkv_bias_other], axis=1)
        bias = jnp.stack([both_bias[0], jnp.zeros_like(both_bias[0]), both_bias[1]])
        bias = jnp.pad(bias, ((0, 5), (0, 0)))
        q, k, v, mixed, lse, attn_cat = attend_forward(attn_in, attn_in_other, attn_full, bias)
        out_full = attn_cat[:, 6 * side :]
        sent = swap(dot_nt(mixed[tokens:], out_full).astype(BF16), "core")
        attn_branch = dot_nt(mixed[:tokens], out_full) + sent.astype(F32) + output_bias
        hidden_resid = residual + attn_branch
        mlp_in, mlp_hat, mlp_inverse = norm(hidden_resid, mlp_gain, mlp_shift)
        mlp_in_other = swap(mlp_in, "core")

        rows8 = lambda b: jnp.broadcast_to(b, (8, hidden))
        act, slope, act_o, slope_o, *down_parts = up_and_down_grads(
            mlp_in,
            mlp_in_other,
            cotangent,
            cot_other,
            up_full,
            rows8(up_bias),
            rows8(up_bias_other),
            order,
            n,
        )
        down_grad = reduce(down_parts)

        pre, pre_o, up_sums, back, back_other = hidden_back(
            cotangent, cot_other, down_full, up_full, slope, slope_o
        )
        grad_mlp_in = back + swap(back_other, "core").astype(F32)
        up_parts = weight_grads(mlp_in, mlp_in_other, pre, pre_o, order, n)
        up_grad = reduce(up_parts)

        grad_out = cotangent.astype(F32)
        norm_grad, mlp_gain_grad, mlp_shift_grad = norm_back(
            grad_mlp_in, mlp_hat, mlp_inverse, mlp_gain
        )
        hidden_grad = grad_out + norm_grad
        grad_attn = hidden_grad.astype(BF16)
        grad_attn_other = swap(grad_attn, "core")

        down_own, down_far = down_full[:, :hidden], down_full[:, hidden:]
        branch = lambda at: dot_nt(act[at], down_own) + dot_nt(act_o[at], down_far)
        sent = swap(branch(slice(tokens, None)).astype(BF16), "core")
        mlp_branch = branch(slice(0, tokens)) + sent.astype(F32) + down_bias
        result = hidden_resid + mlp_branch

        grad_mixed = jnp.concatenate(
            [dot_nn(g, out_full).astype(BF16) for g in (grad_attn, grad_attn_other)]
        )
        dproj = attend_backward(q, k, v, grad_mixed, mixed, lse)
        attn_parts = attention_grads(
            attn_in, attn_in_other, grad_attn, grad_attn_other, dproj, mixed, order, n
        )
        attn_grad = reduce(attn_parts)
        qkv_full = attn_cat[:, : 6 * side]
        sent = swap(dot_nt(dproj[tokens:], qkv_full).astype(BF16), "core")
        grad_attn_in = dot_nt(dproj[:tokens], qkv_full) + sent.astype(F32)
        norm_grad, attn_gain_grad, attn_shift_grad = norm_back(
            grad_attn_in, attn_hat, attn_inverse, attn_gain
        )
        input_grad = hidden_grad + norm_grad
        qkv_grad = attn_grad[:, : 3 * side].reshape(n, 3, side)
        output_grad = attn_grad[:, 3 * side :]

        squares = jnp.stack(
            [
                jnp.sum(result * result),
                jnp.sum(attn_branch * attn_branch),
                jnp.sum(mlp_branch * mlp_branch),
            ]
        )
        common = jnp.concatenate(
            [
                attn_gain_grad,
                attn_shift_grad,
                jnp.sum(grad_attn.astype(F32), axis=0),
                mlp_gain_grad,
                mlp_shift_grad,
                jnp.sum(grad_out, axis=0),
                jnp.pad(squares, (0, 125)),
            ]
        )
        common = common + swap(common, "core")
        proj_sums = jnp.sum(dproj.astype(F32), axis=0)
        own = jnp.concatenate([proj_sums[:side], proj_sums[4 * side : 5 * side], up_sums[0]])
        other = jnp.concatenate([proj_sums[side : 2 * side], proj_sums[5 * side :], up_sums[1]])
        sums = jnp.concatenate([common, own])
        sums = sums + swap(jnp.concatenate([common, other]), "y")
        for axis in reversed(rows):
            sums = sums + swap(sums, axis)
        entry_count = tokens * 2 ** (len(rows) + 2) * width
        vec = [sums[i * width : (i + 1) * width] for i in range(6)]
        rms_values = jnp.sqrt(sums[6 * width : 6 * width + 3] / entry_count)
        tail = sums[6 * width + 128 :]
        return (
            result.astype(BF16),
            input_grad,
            vec[0],
            vec[1],
            qkv_grad,
            tail[: 2 * side].reshape(2, side),
            output_grad,
            vec[2],
            vec[3],
            vec[4],
            up_grad,
            tail[2 * side :],
            down_grad,
            vec[5],
            rms_values,
        )

    return local


def solution(mesh):
    row_size, col_size = mesh.shape["row"], mesh.shape["col"]
    bits = row_size.bit_length() - 1
    rows = tuple(f"r{b}" for b in reversed(range(bits)))
    cube = Mesh(mesh.devices.reshape((2,) * bits + (col_size // 2, 2)), rows + ("y", "core"))
    col = ("y", "core")
    every = rows + col
    placed = (
        P(every, None),
        P(),
        P(),
        P(rows, None, col),
        P(None, col),
        P(rows, col),
        P(),
        P(),
        P(),
        P(rows, col),
        P(col),
        P(rows, col),
        P(),
        P(every, None),
    )
    return jax.shard_map(
        make_local(rows),
        mesh=cube,
        in_specs=placed,
        out_specs=(
            P(every, None),
            P(every, None),
            P(),
            P(),
            P(rows, None, col),
            P(None, col),
            P(rows, col),
            P(),
            P(),
            P(),
            P(rows, col),
            P(col),
            P(rows, col),
            P(),
            P(),
        ),
        check_vma=False,
    )
```

time: 456 us -> 522 us (1.14); the launches traced: 450 us -> 521 us
  Pallas kernels: 55.2 us -> 306 us
  starting transfers between devices: 97.2 us -> 41.4 us
  local copies, waits for them, and re-layouts: 73.1 us -> 19.5 us
  other arithmetic: 68.8 us -> 36.8 us
  matrix products: 57.4 us -> 25.5 us
  waiting for transfers between devices: 95.2 us -> 77.8 us
  between operations: 2.69 us -> 14.6 us
    pallas_call x6 -> x9, Pallas kernels: 55.2 us -> 306 us  [the longest x3 218 us: assemble(): pl.pallas_call(partial(assemble_kernel, rows, xor), in_specs=[anywhere] *...]
    ppermute x30 -> x3, starting transfers between devices: 49.7 us -> 5.68 us  [xor_exchange(): got[bits] = lax.ppermute(blocks_of(bits), axes, perm)]
    slice x44 -> x18, local copies, waits for them, and re-layouts: 33.9 us -> 7.45 us  [the longest x3 1.4 us: reduce_far(): to_low = jnp.concatenate([add(to_low[:half], got_a), to_low[half:]])]
    ppermute x30 -> x3, waiting for transfers between devices: 34.7 us -> 9.56 us  [xor_exchange(): got[bits] = lax.ppermute(blocks_of(bits), axes, perm)]
    dot_general x11 -> x0, matrix products: 20.1 us -> none  [dot_tn(): lax.dot_general(left, right, (((0,), (0,)), ((), ())), preferred_element_...]
    concatenate x13 -> x1, local copies, waits for them, and re-layouts: 20 us -> 0.08 us  [local(): sums = sums + swap(jnp.concatenate([common, other]), 'y')]
    ppermute x54 -> x38, starting transfers between devices: 47.5 us -> 35.5 us  [swap(): return lax.ppermute(array, axis, SWAP)]
    another operation x40 -> x4, other arithmetic: 12 us -> 1.89 us  [the longest x1 1.65 us: local(): both = lax.all_gather(jnp.stack([up_weight, down_weight]), near, axis=0)]
  transfers between devices with their start and end apart: 84 -> 45, of which waited for: 30 -> 20; matrix products, arithmetic and copies ran while one was open for 25% -> 12% of each run, Pallas kernels for 7% -> 56%
where the time goes in v2:
time: 522 us; the launch traced here: 521 us
  Pallas kernels  306 us (59%)
  waiting for transfers between devices  77.8 us (15%)
  starting transfers between devices  41.4 us (8%)
  other arithmetic  36.8 us (7%)
  matrix products  25.5 us (5%)
  local copies, waits for them, and re-layouts  19.5 us (4%)
  between operations  14.6 us (3%)
    pallas_call x3, Pallas kernels, assemble(): pl.pallas_call(partial(assemble_kernel, rows, xor), in_specs=[anywhere] *...  218 us
    ppermute x38, waiting for transfers between devices, swap(): return lax.ppermute(array, axis, SWAP)  59.2 us
    ppermute x38, starting transfers between devices, swap(): return lax.ppermute(array, axis, SWAP)  35.5 us
    pallas_call x1, Pallas kernels, attend_forward(): pl.pallas_call(attend_forward_kernel, grid=(pairs, seq // block), in_spec...  26.2 us
    pallas_call x1, Pallas kernels, attend_backward(): pl.pallas_call(attend_backward_kernel, grid=(pairs, seq // block), in_spe...  21.8 us
    dot_general x8, matrix products, dot_nt(): lax.dot_general(left, right, (((1,), (1,)), ((), ())), preferred_element_...  21.6 us
    pallas_call x1, Pallas kernels, up_and_down_grads(): pl.pallas_call(partial(up_kernel, rows, n), grid=(steps,), in_specs=[whol...  13.6 us
    pallas_call x1, Pallas kernels, hidden_back(): pl.pallas_call(hidden_back_kernel, grid=(steps,), in_specs=[whole(ga.shap...  11.6 us
  transfers between devices with their start and end apart: 45, of which 20 were waited for; matrix products, arithmetic and copies ran while one was open for 12% of the time, Pallas kernels for 56%

profile of v2, /device:TPU:0, one launch (start us, length us, event | category | flops | bytes accessed | tf_op | source)
XLA Modules:
  0.0 521.5 jit_solution(16563677630654758143)
XLA Ops:
  9.5 3.1 collective-permute-start.1
  12.5 2.6 collective-permute-start.2
  18.4 8.1 %collective-permute-done.2 = bf16[96,768]{1,0:T(8,128)(2,1)S(1)} collective-permute-done((bf16[96,768]{1,0:T(8,128)(2,1)S(1)}, bf16[96,768]{1,0:T(8,128)(2,1)S(1)}, u32[]{:S(2)}, u32[]{:S(2)}) %collective-permute-start.2) | collective-permute-done | bytes 147488 | tf_op jit(solution)/shard_map/ppermute | solution.py:41
  30.9 1.7 pad_maximum_fusion.8
  32.7 9.0 %collective-permute-done.8 = f32[1152]{0:T(1024)S(1)} collective-permute-done((f32[1152]{0:T(1024)S(1)}, f32[1152]{0:T(1024)S(1)}, u32[]{:S(2)}, u32[]{:S(2)}) %collective-permute-start.8) | collective-permute-done | bytes 4640 | tf_op jit(solution)/shard_map/ppermute | solution.py:20
  41.8 1.6 collective-permute-start.6
  44.8 3.9 collective-permute-done.6.a_ref
  48.7 1.6 collective-permute-done.7.b_ref
  50.3 72.7 %assemble.3.w_ref = bf16[768,1536]{1,0:T(8,128)(2,1)} custom-call(bf16[4,96,768]{2,1,0:T(8,128)(2,1)} %copy-done.3, bf16[4,96,768]{2,1,0:T(8,128)(2,1)} %copy-done.14, bf16[4,96,768]{2,1,0:T(8,128)(2,1)} %copy-done.15, bf16[2,96,768]{2,1,0:T(8,128)(2,1)} %collective-permute-done.6.a_ref, bf16[2,96,768]{2,1,0:T(8,128)(2,1)} %collective-permute-done.7.b_ref), custom_call_target="tpu_custom_call" | custom-call | bytes 9437184 | tf_op jit(solution)/shard_map/assemble/pallas_call | solution.py:161
  123.1 26.2 %attend_forward.1 = (bf16[3,1024,128]{2,1,0:T(8,128)(2,1)}, bf16[3,1024,128]{2,1,0:T(8,128)(2,1)}, bf16[3,1024,128]{2,1,0:T(8,128)(2,1)}, bf16[1024,384]{1,0:T(8...) custom-call(bf16[512,768]{1,0:T(8,128)(2,1)} %copy-done.17, bf16[512,768]{1,0:T(8,128)(2,1)} %collective-permute-done.xb_ref, ...), custom_call_target="tpu_custom_call" | custom-call | flops 9663676416 | bytes 12582912 | tf_op jit(solution)/shard_map/attend_forward/pallas_call | solution.py:297
  149.3 1.8 convolution_convert_fusion
  158.0 2.9 fusion.58
  162.8 6.5 %collective-permute-done.12.x_ref = bf16[4,96,768]{2,1,0:T(8,128)(2,1)S(1)} collective-permute-done((bf16[4,96,768]{2,1,0:T(8,128)(2,1)S(1)}, bf16[4,96,768]{2,1,0:T(8,128)(2,1)S(1)}, u32[]{:S(2)}, u32[]{:S(2)}) %collective-permute-start.12) | collective-permute-done | bytes 589856 | tf_op jit(solution)/shard_map/ppermute | solution.py:20
  170.4 10.6 %collective-permute-done.16.x_ref = bf16[4,96,768]{2,1,0:T(8,128)(2,1)S(1)} collective-permute-done((bf16[4,96,768]{2,1,0:T(8,128)(2,1)S(1)}, bf16[4,96,768]{2,1,0:T(8,128)(2,1)S(1)}, u32[]{:S(2)}, u32[]{:S(2)}) %collective-permute-start.16) | collective-permute-done | bytes 589856 | tf_op jit(solution)/shard_map/ppermute | solution.py:20
  184.1 4.7 collective-permute-done.14.a_ref
  191.6 72.7 %assemble.4.w_ref.wo_ref.u_ref.uo_ref = bf16[768,1536]{1,0:T(8,128)(2,1)} custom-call(bf16[4,96,768]{2,1,0:T(8,128)(2,1)} %copy-done.5, bf16[4,96,768]{2,1,0:T(8,128)(2,1)} %copy-done.11, bf16[4,96,768]{2,1,0:T(8,128)(2,1)} %copy-done.13, bf16[2,96,768]{2,1,0:T(8,128)(2,1)} %copy-done.24, bf16[2,96,768]{2,1,0:T(8,128)(2,1)} %collective-permute-done.15.b_ref), custom_call_target="tpu_custom_call" | custom-call | bytes 9437184 | tf_op jit(solution)/shard_map/assemble/pallas_call | solution.py:161
  264.4 72.7 %assemble.5.w_ref.wo_ref = bf16[768,1536]{1,0:T(8,128)(2,1)} custom-call(bf16[4,96,768]{2,1,0:T(8,128)(2,1)} %copy-done.4, bf16[4,96,768]{2,1,0:T(8,128)(2,1)} %copy-done.10, bf16[4,96,768]{2,1,0:T(8,128)(2,1)} %copy-done.12, bf16[2,96,768]{2,1,0:T(8,128)(2,1)} %collective-permute-done.18.a_ref, bf16[2,96,768]{2,1,0:T(8,128)(2,1)} %collective-permute-done.19.b_ref), custom_call_target="tpu_custom_call" | custom-call | bytes 9437184 | tf_op jit(solution)/shard_map/assemble/pallas_call | solution.py:161
  338.3 13.6 %up_and_down_grads.1 = (bf16[1024,768]{1,0:T(8,128)(2,1)}, bf16[1024,768]{1,0:T(8,128)(2,1)}, bf16[1024,768]{1,0:T(8,128)(2,1)}, bf16[1024,768]{1,0:T(8,128)(2,1...) custom-call(bf16[512,768]{1,0:T(8,128)(2,1)} %add_convert_fusion.1.x, ...), custom_call_target="tpu_custom_call" | custom-call | flops 4831838208 | bytes 9437184 | tf_op jit(solution)/shard_map/up_and_down_grads/pallas_call | solution.py:474
  352.0 3.7 fusion.33
  355.7 3.2 fusion.31
  359.9 11.6 %hidden_back.1 = (bf16[1024,768]{1,0:T(8,128)(2,1)}, bf16[1024,768]{1,0:T(8,128)(2,1)}, f32[8,768]{1,0:T(8,128)}, f32[512,768]{1,0:T(8,128)}, bf16[512,768]{1,0:T(8,128)(2,1)}) custom-call(bf16[512,768]{1,0:T(8,128)(2,1)} %ga_ref.3, bf16[512,768]{1,0:T(8,128)(2,1)} %collective-permute-done.11.gb_ref, bf16[768,1536]{1,0:T(8,128)(2,1)} %assemble.5.w_ref.wo_ref, ...), custom_call_target="tpu_custom_call" | custom-call | flops 4831838208 | bytes 9437184 | tf_op jit(solution)/shard_map/hidden_back/pallas_call | solution.py:534
  371.5 6.4 %weight_grads.1 = (bf16[384,768]{1,0:T(8,128)(2,1)}, bf16[384,768]{1,0:T(8,128)(2,1)}, bf16[384,768]{1,0:T(8,128)(2,1)}, bf16[192,768]{1,0:T(8,128)(2,1)}, bf16[192,768]{1,0:T(8,128)(2,1)}) custom-call(bf16[512,768]{1,0:T(8,128)(2,1)} %add_convert_fusion.1.xa_ref, bf16[512,768]{1,0:T(8,128)(2,1)} %collective-permute-done.10.xb_ref, ...), custom_call_target="tpu_custom_call" | custom-call | flops 2415919104 | bytes 4718592 | tf_op jit(solution)/shard_map/weight_grads/pallas_call | solution.py:586
  377.9 1.6 collective-permute-start.33
  380.9 3.0 add_convert_fusion
  395.2 2.9 multiply_reduce_fusion.3
  398.1 7.0 %collective-permute-done.38 = bf16[4,96,768]{2,1,0:T(8,128)(2,1)S(1)} collective-permute-done((bf16[4,96,768]{2,1,0:T(8,128)(2,1)S(1)}, bf16[4,96,768]{2,1,0:T(8,128)(2,1)S(1)}, u32[]{:S(2)}, u32[]{:S(2)}) %collective-permute-start.38) | collective-permute-done | bytes 589856 | tf_op jit(solution)/shard_map/ppermute | solution.py:20
  407.1 5.3 %convert_reduce_fusion.3 = (f32[768]{0:T(1024)}, bf16[512,768]{1,0:T(8,128)(2,1)}, f32[512,768]{1,0:T(8,128)}, bf16[512,768]{1,0:T(8,128)(2,1)}, f32[768]{0:T(1024)}) fusion(f32[512]{0:T(512)S(1)} %get-tuple-element.169, f32[512,768]{1,0:T(8,128)S(1)} %get-tuple-element.137, f32[512]{0:T(512)S(1)} %broadcast_multiply_fusion.4, ...), kind=kLoop, calls=%fused_computation.24 | loop fusion | flops 6683136 | bytes 9454592 | tf_op jit(solution)/shard_map/reduce_sum | solution.py:754
  413.2 1.9 convolution_convert_fusion.2
  415.1 2.0 collective-permute-done.34
  417.6 2.3 fusion.28
  420.0 1.9 convolution_convert_fusion.1
  422.9 21.8 %attend_backward.1.dproj_ref = bf16[1024,1152]{1,0:T(8,128)(2,1)} custom-call(bf16[3,1024,128]{2,1,0:T(8,128)(2,1)} %get-tuple-element.53.q_ref, bf16[3,1024,128]{2,1,0:T(8,128)(2,1)} %get-tuple-element.54.k_ref, bf16[3,1024,128]{2,1,0:T(8,128)(2,1)} %get-tuple-element.55.v_ref, bf16[1024,384]{1,0:T(8,128)(2,1)} %pad_maximum_fusion.grad_ref, ...), custom_call_target="tpu_custom_call" | custom-call | flops 20132659200 | bytes 7864320 | tf_op jit(solution)/shard_map/attend_backward/pallas_call | solution.py:376
  444.7 3.1 fusion.20
  447.8 8.2 %attention_grads.1 = (bf16[384,768]{1,0:T(8,128)(2,1)}, bf16[384,768]{1,0:T(8,128)(2,1)}, bf16[384,768]{1,0:T(8,128)(2,1)}, bf16[192,768]{1,0:T(8,128)(2,1)}, bf16[192,768]{1,0:T(8,128)(2,1)}) custom-call(bf16[512,768]{1,0:T(8,128)(2,1)} %copy-done.17, bf16[512,768]{1,0:T(8,128)(2,1)} %collective-permute-done.xb_ref, ...), custom_call_target="tpu_custom_call" | custom-call | flops 2415919104 | bytes 4718592 | tf_op jit(solution)/shard_map/attention_grads/pallas_call | solution.py:424
  459.4 1.6 collective-permute-start.31
  461.0 4.5 collective-permute-done.29
  467.2 2.1 collective-permute-done.31
  469.5 1.6 collective-permute-start.32
  471.1 3.3 fusion.12
  474.5 2.0 constant_dynamic-update-slice_fusion
  478.3 1.6 convert_element_type.239
  479.9 1.6 convert_element_type.225
  481.6 3.0 collective-permute-done.25
  486.7 2.5 fusion.30
  490.6 2.6 collective-permute-start.27
  495.1 3.2 collective-permute-start.28
  498.3 3.1 fusion.11
  503.3 8.9 %reduce-scatter.4.cloned.1.call-done = bf16[96,768]{1,0:T(8,128)(2,1)} async-done(((bf16[384,768]{1,0:T(8,128)(2,1)}), bf16[96,768]{1,0:T(8,128)(2,1)}) %reduce-scatter.4.cloned.1.call-update) | async-done | bytes 147472 | tf_op jit(solution)/shard_map/reduce_scatter | solution.py:190
  (262 shorter events, 63.3 us)
Async XLA Ops:
  7.2 144.4 %all-gather.3.cloned.1.call-start = ((), (), s32[]{:S(2)}) async-start(), calls=%async_computation.6 | async-start | bytes 1474560 | tf_op jit(solution)/shard_map/all_gather | solution.py:671
  9.5 8.9 %collective-permute-start.1 = (bf16[96,768]{1,0:T(8,128)(2,1)S(1)}, bf16[96,768]{1,0:T(8,128)(2,1)S(1)}, u32[]{:S(2)}, u32[]{:S(2)}) collective-permute-start(bf16[96,768]{1,0:T(8,128)(2,1)S(1)} %pad_maximum_fusion.9), channel_id=1, source_target_pairs={{0,8},{8,0},{16,24},{24,16},{1,9},{9,1},{17,25},{25,17},{2,10},{10... | collective-permute-start | bytes 442376 | tf_op jit(solution)/shard_map/ppermute | solution.py:41
  12.5 14.0 %collective-permute-start.2 = (bf16[96,768]{1,0:T(8,128)(2,1)S(1)}, bf16[96,768]{1,0:T(8,128)(2,1)S(1)}, u32[]{:S(2)}, u32[]{:S(2)}) collective-permute-start(bf16[96,768]{1,0:T(8,128)(2,1)S(1)} %pad_maximum_fusion.9), channel_id=1, source_target_pairs={{0,16},{8,24},{16,0},{24,8},{1,17},{9,25},{17,1},{25,9},{2,18},{10... | collective-permute-start | bytes 442376 | tf_op jit(solution)/shard_map/ppermute | solution.py:41
  15.1 11.4 %collective-permute-start.3 = (bf16[96,768]{1,0:T(8,128)(2,1)S(1)}, bf16[96,768]{1,0:T(8,128)(2,1)S(1)}, u32[]{:S(2)}, u32[]{:S(2)}) collective-permute-start(bf16[96,768]{1,0:T(8,128)(2,1)S(1)} %pad_maximum_fusion.9), channel_id=1, source_target_pairs={{0,24},{8,16},{16,8},{24,0},{1,25},{9,17},{17,9},{25,1},{2,26},{10... | collective-permute-start | bytes 442376 | tf_op jit(solution)/shard_map/ppermute | solution.py:41
  26.6 15.1 %collective-permute-start.4 = (bf16[4,96,768]{2,1,0:T(8,128)(2,1)S(1)}, bf16[4,96,768]{2,1,0:T(8,128)(2,1)S(1)}, u32[]{:S(2)}, u32[]{:S(2)}) collective-permute-start(bf16[4,96,768]{2,1,0:T(8,128)(2,1)S(1)} %pad_maximum_fusion.1.s_ref), channel_id=1, source_target_pairs={{0,4},{4,0},{1,5},{5,1},{2,6},{6,2},{3,7},{7,3},{8,12},{12,8},{9,1... | collective-permute-start | bytes 1769480 | tf_op jit(solution)/shard_map/ppermute | solution.py:20
  28.2 15.2 %collective-permute-start.5 = (bf16[4,96,768]{2,1,0:T(8,128)(2,1)S(1)}, bf16[4,96,768]{2,1,0:T(8,128)(2,1)S(1)}, u32[]{:S(2)}, u32[]{:S(2)}) collective-permute-start(bf16[4,96,768]{2,1,0:T(8,128)(2,1)S(1)} %pad_maximum_fusion.1.s_ref), channel_id=1, source_target_pairs={{0,2},{2,0},{1,3},{3,1},{4,6},{6,4},{5,7},{7,5},{8,10},{10,8},{9,1... | collective-permute-start | bytes 1769480 | tf_op jit(solution)/shard_map/ppermute | solution.py:20
  30.1 93.0 %copy-start.17 = (bf16[512,768]{1,0:T(8,128)(2,1)}, bf16[512,768]{1,0:T(8,128)(2,1)S(1)}, u32[]{:S(2)}) copy-start(bf16[512,768]{1,0:T(8,128)(2,1)S(1)} %fusion.7.xa_ref) | copy-start | bytes 2359300
  30.1 93.0 %collective-permute-start = (bf16[512,768]{1,0:T(8,128)(2,1)S(1)}, bf16[512,768]{1,0:T(8,128)(2,1)}, u32[]{:S(2)}, u32[]{:S(2)}) collective-permute-start(bf16[512,768]{1,0:T(8,128)(2,1)S(1)} %fusion.7.xa_ref), channel_id=1, source_target_pairs={{0,1},{1,0},{2,3},{3,2},{4,5},{5,4},{6,7},{7,6},{8,9},{9,8},{10,11... | collective-permute-start | bytes 2359304 | tf_op jit(solution)/shard_map/ppermute | solution.py:20
  30.3 11.4 %collective-permute-start.8 = (f32[1152]{0:T(1024)S(1)}, f32[1152]{0:T(1024)S(1)}, u32[]{:S(2)}, u32[]{:S(2)}) collective-permute-start(f32[1152]{0:T(1024)S(1)} %pad_maximum_fusion.10), channel_id=1, source_target_pairs={{0,2},{2,0},{1,3},{3,1},{4,6},{6,4},{5,7},{7,5},{8,10},{10,8},{9,1... | collective-permute-start | bytes 13832 | tf_op jit(solution)/shard_map/ppermute | solution.py:20
  32.5 445.7 %reduce-scatter.8.cloned.1.call-start = ((), (), s32[]{:S(2)}) async-start(), calls=%async_computation.5 | async-start | bytes 737280 | tf_op jit(solution)/shard_map/reduce_scatter | solution.py:190
  41.7 81.4 %copy-start.42 = (f32[1152]{0:T(1024)}, f32[1152]{0:T(1024)S(1)}, u32[]{:S(2)}) copy-start(f32[1152]{0:T(1024)S(1)} %collective-permute-done.8) | copy-start | bytes 13828
  41.8 6.9 %collective-permute-start.6 = (bf16[2,96,768]{2,1,0:T(8,128)(2,1)S(1)}, bf16[2,96,768]{2,1,0:T(8,128)(2,1)}, u32[]{:S(2)}, u32[]{:S(2)}) collective-permute-start(bf16[2,96,768]{2,1,0:T(8,128)(2,1)S(1)} %slice.253), channel_id=1, source_target_pairs={{0,2},{2,0},{1,3},{3,1},{4,6},{6,4},{5,7},{7,5},{8,10},{10,8},{9,1... | collective-permute-start | bytes 884744 | tf_op jit(solution)/shard_map/ppermute | solution.py:20
  43.4 6.9 %collective-permute-start.7 = (bf16[2,96,768]{2,1,0:T(8,128)(2,1)S(1)}, bf16[2,96,768]{2,1,0:T(8,128)(2,1)}, u32[]{:S(2)}, u32[]{:S(2)}) collective-permute-start(bf16[2,96,768]{2,1,0:T(8,128)(2,1)S(1)} %slice.254), channel_id=1, source_target_pairs={{0,4},{4,0},{1,5},{5,1},{2,6},{6,2},{3,7},{7,3},{8,12},{12,8},{9,1... | collective-permute-start | bytes 884744 | tf_op jit(solution)/shard_map/ppermute | solution.py:20
  151.1 4.5 collective-permute-start.9
  151.2 186.0 %collective-permute-start.11 = (bf16[512,768]{1,0:T(8,128)(2,1)}, bf16[512,768]{1,0:T(8,128)(2,1)}, u32[]{:S(2)}, u32[]{:S(2)}) collective-permute-start(bf16[512,768]{1,0:T(8,128)(2,1)} %ga_ref.3), channel_id=1, source_target_pairs={{0,1},{1,0},{2,3},{3,2},{4,5},{5,4},{6,7},{7,6},{8,9},{9,8},{10,11... | collective-permute-start | bytes 2359304 | tf_op jit(solution)/shard_map/ppermute | solution.py:20
  153.0 16.2 %collective-permute-start.12 = (bf16[4,96,768]{2,1,0:T(8,128)(2,1)S(1)}, bf16[4,96,768]{2,1,0:T(8,128)(2,1)S(1)}, u32[]{:S(2)}, u32[]{:S(2)}) collective-permute-start(bf16[4,96,768]{2,1,0:T(8,128)(2,1)S(1)} %get-tuple-element.140.s_ref), channel_id=1, source_target_pairs={{0,4},{4,0},{1,5},{5,1},{2,6},{6,2},{3,7},{7,3},{8,12},{12,8},{9,1... | collective-permute-start | bytes 1769480 | tf_op jit(solution)/shard_map/ppermute | solution.py:20
  153.6 16.2 %collective-permute-start.13 = (bf16[4,96,768]{2,1,0:T(8,128)(2,1)S(1)}, bf16[4,96,768]{2,1,0:T(8,128)(2,1)S(1)}, u32[]{:S(2)}, u32[]{:S(2)}) collective-permute-start(bf16[4,96,768]{2,1,0:T(8,128)(2,1)S(1)} %get-tuple-element.140.s_ref), channel_id=1, source_target_pairs={{0,2},{2,0},{1,3},{3,1},{4,6},{6,4},{5,7},{7,5},{8,10},{10,8},{9,1... | collective-permute-start | bytes 1769480 | tf_op jit(solution)/shard_map/ppermute | solution.py:20
  154.1 26.9 %collective-permute-start.16 = (bf16[4,96,768]{2,1,0:T(8,128)(2,1)S(1)}, bf16[4,96,768]{2,1,0:T(8,128)(2,1)S(1)}, u32[]{:S(2)}, u32[]{:S(2)}) collective-permute-start(bf16[4,96,768]{2,1,0:T(8,128)(2,1)S(1)} %get-tuple-element.141.s_ref), channel_id=1, source_target_pairs={{0,4},{4,0},{1,5},{5,1},{2,6},{6,2},{3,7},{7,3},{8,12},{12,8},{9,1... | collective-permute-start | bytes 1769480 | tf_op jit(solution)/shard_map/ppermute | solution.py:20
  156.5 26.0 %collective-permute-start.17 = (bf16[4,96,768]{2,1,0:T(8,128)(2,1)S(1)}, bf16[4,96,768]{2,1,0:T(8,128)(2,1)S(1)}, u32[]{:S(2)}, u32[]{:S(2)}) collective-permute-start(bf16[4,96,768]{2,1,0:T(8,128)(2,1)S(1)} %get-tuple-element.141.s_ref), channel_id=1, source_target_pairs={{0,2},{2,0},{1,3},{3,1},{4,6},{6,4},{5,7},{7,5},{8,10},{10,8},{9,1... | collective-permute-start | bytes 1769480 | tf_op jit(solution)/shard_map/ppermute | solution.py:20
  169.3 167.9 %collective-permute-start.10 = (bf16[512,768]{1,0:T(8,128)(2,1)}, bf16[512,768]{1,0:T(8,128)(2,1)}, u32[]{:S(2)}, u32[]{:S(2)}) collective-permute-start(bf16[512,768]{1,0:T(8,128)(2,1)} %add_convert_fusion.1.xa_ref), channel_id=1, source_target_pairs={{0,1},{1,0},{2,3},{3,2},{4,5},{5,4},{6,7},{7,6},{8,9},{9,8},{10,11... | collective-permute-start | bytes 2359304 | tf_op jit(solution)/shard_map/ppermute | solution.py:20
  169.8 19.0 %collective-permute-start.14 = (bf16[2,96,768]{2,1,0:T(8,128)(2,1)S(1)}, bf16[2,96,768]{2,1,0:T(8,128)(2,1)S(1)}, u32[]{:S(2)}, u32[]{:S(2)}) collective-permute-start(bf16[2,96,768]{2,1,0:T(8,128)(2,1)S(1)} %slice.259), channel_id=1, source_target_pairs={{0,2},{2,0},{1,3},{3,1},{4,6},{6,4},{5,7},{7,5},{8,10},{10,8},{9,1... | collective-permute-start | bytes 884744 | tf_op jit(solution)/shard_map/ppermute | solution.py:20
  181.0 83.3 %copy-start.10 = (bf16[4,96,768]{2,1,0:T(8,128)(2,1)}, bf16[4,96,768]{2,1,0:T(8,128)(2,1)S(1)}, u32[]{:S(2)}) copy-start(bf16[4,96,768]{2,1,0:T(8,128)(2,1)S(1)} %collective-permute-done.16.x_ref) | copy-start | bytes 1769476
  181.0 10.6 %collective-permute-start.15 = (bf16[2,96,768]{2,1,0:T(8,128)(2,1)S(1)}, bf16[2,96,768]{2,1,0:T(8,128)(2,1)}, u32[]{:S(2)}, u32[]{:S(2)}) collective-permute-start(bf16[2,96,768]{2,1,0:T(8,128)(2,1)S(1)} %slice.260), channel_id=1, source_target_pairs={{0,4},{4,0},{1,5},{5,1},{2,6},{6,2},{3,7},{7,3},{8,12},{12,8},{9,1... | collective-permute-start | bytes 884744 | tf_op jit(solution)/shard_map/ppermute | solution.py:20
  182.5 81.9 %collective-permute-start.18 = (bf16[2,96,768]{2,1,0:T(8,128)(2,1)}, bf16[2,96,768]{2,1,0:T(8,128)(2,1)}, u32[]{:S(2)}, u32[]{:S(2)}) collective-permute-start(bf16[2,96,768]{2,1,0:T(8,128)(2,1)} %slice.263), channel_id=1, source_target_pairs={{0,2},{2,0},{1,3},{3,1},{4,6},{6,4},{5,7},{7,5},{8,10},{10,8},{9,1... | collective-permute-start | bytes 884744 | tf_op jit(solution)/shard_map/ppermute | solution.py:20
  189.5 74.9 %collective-permute-start.19 = (bf16[2,96,768]{2,1,0:T(8,128)(2,1)}, bf16[2,96,768]{2,1,0:T(8,128)(2,1)}, u32[]{:S(2)}, u32[]{:S(2)}) collective-permute-start(bf16[2,96,768]{2,1,0:T(8,128)(2,1)} %slice.264), channel_id=1, source_target_pairs={{0,4},{4,0},{1,5},{5,1},{2,6},{6,2},{3,7},{7,3},{8,12},{12,8},{9,1... | collective-permute-start | bytes 884744 | tf_op jit(solution)/shard_map/ppermute | solution.py:20
  358.9 27.9 %collective-permute-start.37 = (bf16[2,96,768]{2,1,0:T(8,128)(2,1)S(1)}, bf16[2,96,768]{2,1,0:T(8,128)(2,1)S(1)}, u32[]{:S(2)}, u32[]{:S(2)}) collective-permute-start(bf16[2,96,768]{2,1,0:T(8,128)(2,1)S(1)} %bitcast.84), channel_id=1, source_target_pairs={{0,2},{2,0},{1,3},{3,1},{4,6},{6,4},{5,7},{7,5},{8,10},{10,8},{9,1... | collective-permute-start | bytes 884744 | tf_op jit(solution)/shard_map/ppermute | solution.py:20
  359.4 29.5 %collective-permute-start.39 = (bf16[2,96,768]{2,1,0:T(8,128)(2,1)}, bf16[2,96,768]{2,1,0:T(8,128)(2,1)S(1)}, u32[]{:S(2)}, u32[]{:S(2)}) collective-permute-start(bf16[2,96,768]{2,1,0:T(8,128)(2,1)} %bitcast.36), channel_id=1, source_target_pairs={{0,4},{4,0},{1,5},{5,1},{2,6},{6,2},{3,7},{7,3},{8,12},{12,8},{9,1... | collective-permute-start | bytes 884744 | tf_op jit(solution)/shard_map/ppermute | solution.py:20
  377.9 11.8 %collective-permute-start.33 = (bf16[2,96,768]{2,1,0:T(8,128)(2,1)}, bf16[2,96,768]{2,1,0:T(8,128)(2,1)S(1)}, u32[]{:S(2)}, u32[]{:S(2)}) collective-permute-start(bf16[2,96,768]{2,1,0:T(8,128)(2,1)} %bitcast.85), channel_id=1, source_target_pairs={{0,2},{2,0},{1,3},{3,1},{4,6},{6,4},{5,7},{7,5},{8,10},{10,8},{9,1... | collective-permute-start | bytes 884744 | tf_op jit(solution)/shard_map/ppermute | solution.py:20
  379.4 11.8 %collective-permute-start.35 = (bf16[2,96,768]{2,1,0:T(8,128)(2,1)}, bf16[2,96,768]{2,1,0:T(8,128)(2,1)S(1)}, u32[]{:S(2)}, u32[]{:S(2)}) collective-permute-start(bf16[2,96,768]{2,1,0:T(8,128)(2,1)} %bitcast.83), channel_id=1, source_target_pairs={{0,4},{4,0},{1,5},{5,1},{2,6},{6,2},{3,7},{7,3},{8,12},{12,8},{9,1... | collective-permute-start | bytes 884744 | tf_op jit(solution)/shard_map/ppermute | solution.py:20
  383.9 9.7 %collective-permute-start.20 = (bf16[512,768]{1,0:T(8,128)(2,1)S(1)}, bf16[512,768]{1,0:T(8,128)(2,1)S(1)}, u32[]{:S(2)}, u32[]{:S(2)}) collective-permute-start(bf16[512,768]{1,0:T(8,128)(2,1)S(1)} %add_convert_fusion), channel_id=1, source_target_pairs={{0,1},{1,0},{2,3},{3,2},{4,5},{5,4},{6,7},{7,6},{8,9},{9,8},{10,11... | collective-permute-start | bytes 2359304 | tf_op jit(solution)/shard_map/ppermute | solution.py:20
  387.5 7.7 %collective-permute-start.21 = (bf16[512,768]{1,0:T(8,128)(2,1)S(1)}, bf16[512,768]{1,0:T(8,128)(2,1)S(1)}, u32[]{:S(2)}, u32[]{:S(2)}) collective-permute-start(bf16[512,768]{1,0:T(8,128)(2,1)S(1)} %copy-done.47), channel_id=1, source_target_pairs={{0,1},{1,0},{2,3},{3,2},{4,5},{5,4},{6,7},{7,6},{8,9},{9,8},{10,11... | collective-permute-start | bytes 2359304 | tf_op jit(solution)/shard_map/ppermute | solution.py:20
  388.9 16.2 %collective-permute-start.38 = (bf16[4,96,768]{2,1,0:T(8,128)(2,1)S(1)}, bf16[4,96,768]{2,1,0:T(8,128)(2,1)S(1)}, u32[]{:S(2)}, u32[]{:S(2)}) collective-permute-start(bf16[4,96,768]{2,1,0:T(8,128)(2,1)S(1)} %pad_maximum_fusion.6), channel_id=1, source_target_pairs={{0,4},{4,0},{1,5},{5,1},{2,6},{6,2},{3,7},{7,3},{8,12},{12,8},{9,1... | collective-permute-start | bytes 1769480 | tf_op jit(solution)/shard_map/ppermute | solution.py:20
  389.7 16.3 %collective-permute-start.40 = (bf16[4,96,768]{2,1,0:T(8,128)(2,1)S(1)}, bf16[4,96,768]{2,1,0:T(8,128)(2,1)S(1)}, u32[]{:S(2)}, u32[]{:S(2)}) collective-permute-start(bf16[4,96,768]{2,1,0:T(8,128)(2,1)S(1)} %pad_maximum_fusion.7), channel_id=1, source_target_pairs={{0,2},{2,0},{1,3},{3,1},{4,6},{6,4},{5,7},{7,5},{8,10},{10,8},{9,1... | collective-permute-start | bytes 1769480 | tf_op jit(solution)/shard_map/ppermute | solution.py:20
  391.2 25.9 %collective-permute-start.34 = (bf16[4,96,768]{2,1,0:T(8,128)(2,1)}, bf16[4,96,768]{2,1,0:T(8,128)(2,1)}, u32[]{:S(2)}, u32[]{:S(2)}) collective-permute-start(bf16[4,96,768]{2,1,0:T(8,128)(2,1)} %pad_maximum_fusion.4), channel_id=1, source_target_pairs={{0,4},{4,0},{1,5},{5,1},{2,6},{6,2},{3,7},{7,3},{8,12},{12,8},{9,1... | collective-permute-start | bytes 1769480 | tf_op jit(solution)/shard_map/ppermute | solution.py:20
  393.6 24.0 %collective-permute-start.36 = (bf16[4,96,768]{2,1,0:T(8,128)(2,1)}, bf16[4,96,768]{2,1,0:T(8,128)(2,1)}, u32[]{:S(2)}, u32[]{:S(2)}) collective-permute-start(bf16[4,96,768]{2,1,0:T(8,128)(2,1)} %pad_maximum_fusion.5), channel_id=1, source_target_pairs={{0,2},{2,0},{1,3},{3,1},{4,6},{6,4},{5,7},{7,5},{8,10},{10,8},{9,1... | collective-permute-start | bytes 1769480 | tf_op jit(solution)/shard_map/ppermute | solution.py:20
  407.0 72.9 %reduce-scatter.6.cloned.1.call-start = ((), (), s32[]{:S(2)}) async-start(), calls=%async_computation.4 | async-start | bytes 737280 | tf_op jit(solution)/shard_map/reduce_scatter | solution.py:190
  412.4 7.6 %collective-permute-start.22 = (bf16[512,768]{1,0:T(8,128)(2,1)}, bf16[512,768]{1,0:T(8,128)(2,1)S(1)}, u32[]{:S(2)}, u32[]{:S(2)}) collective-permute-start(bf16[512,768]{1,0:T(8,128)(2,1)} %get-tuple-element.133.ga_ref), channel_id=1, source_target_pairs={{0,1},{1,0},{2,3},{3,2},{4,5},{5,4},{6,7},{7,6},{8,9},{9,8},{10,11... | collective-permute-start | bytes 2359304 | tf_op jit(solution)/shard_map/ppermute | solution.py:20
  420.0 92.2 %reduce-scatter.4.cloned.1.call-start = ((), (), s32[]{:S(2)}) async-start(), calls=%async_computation.3 | async-start | bytes 737280 | tf_op jit(solution)/shard_map/reduce_scatter | solution.py:190
  457.2 8.3 %collective-permute-start.29 = (bf16[2,96,768]{2,1,0:T(8,128)(2,1)}, bf16[2,96,768]{2,1,0:T(8,128)(2,1)S(1)}, u32[]{:S(2)}, u32[]{:S(2)}) collective-permute-start(bf16[2,96,768]{2,1,0:T(8,128)(2,1)} %bitcast.87), channel_id=1, source_target_pairs={{0,2},{2,0},{1,3},{3,1},{4,6},{6,4},{5,7},{7,5},{8,10},{10,8},{9,1... | collective-permute-start | bytes 884744 | tf_op jit(solution)/shard_map/ppermute | solution.py:20
  458.9 12.1 %collective-permute-start.23 = (bf16[512,768]{1,0:T(8,128)(2,1)S(1)}, bf16[512,768]{1,0:T(8,128)(2,1)S(1)}, u32[]{:S(2)}, u32[]{:S(2)}) collective-permute-start(bf16[512,768]{1,0:T(8,128)(2,1)S(1)} %fusion.20), channel_id=1, source_target_pairs={{0,1},{1,0},{2,3},{3,2},{4,5},{5,4},{6,7},{7,6},{8,9},{9,8},{10,11... | collective-permute-start | bytes 2359304 | tf_op jit(solution)/shard_map/ppermute | solution.py:20
  459.4 9.9 %collective-permute-start.31 = (bf16[2,96,768]{2,1,0:T(8,128)(2,1)S(1)}, bf16[2,96,768]{2,1,0:T(8,128)(2,1)S(1)}, u32[]{:S(2)}, u32[]{:S(2)}) collective-permute-start(bf16[2,96,768]{2,1,0:T(8,128)(2,1)S(1)} %bitcast.86), channel_id=1, source_target_pairs={{0,4},{4,0},{1,5},{5,1},{2,6},{6,2},{3,7},{7,3},{8,12},{12,8},{9,1... | collective-permute-start | bytes 884744 | tf_op jit(solution)/shard_map/ppermute | solution.py:20
  465.7 21.0 %collective-permute-start.30 = (bf16[4,96,768]{2,1,0:T(8,128)(2,1)S(1)}, bf16[4,96,768]{2,1,0:T(8,128)(2,1)}, u32[]{:S(2)}, u32[]{:S(2)}) collective-permute-start(bf16[4,96,768]{2,1,0:T(8,128)(2,1)S(1)} %pad_maximum_fusion.2), channel_id=1, source_target_pairs={{0,4},{4,0},{1,5},{5,1},{2,6},{6,2},{3,7},{7,3},{8,12},{12,8},{9,1... | collective-permute-start | bytes 1769480 | tf_op jit(solution)/shard_map/ppermute | solution.py:20
  469.5 17.3 %collective-permute-start.32 = (bf16[4,96,768]{2,1,0:T(8,128)(2,1)S(1)}, bf16[4,96,768]{2,1,0:T(8,128)(2,1)}, u32[]{:S(2)}, u32[]{:S(2)}) collective-permute-start(bf16[4,96,768]{2,1,0:T(8,128)(2,1)S(1)} %pad_maximum_fusion.3), channel_id=1, source_target_pairs={{0,2},{2,0},{1,3},{3,1},{4,6},{6,4},{5,7},{7,5},{8,10},{10,8},{9,1... | collective-permute-start | bytes 1769480 | tf_op jit(solution)/shard_map/ppermute | solution.py:20
  476.5 1.2 collective-permute-start.24
  477.8 6.8 %collective-permute-start.25 = (f32[5888]{0:T(1024)S(1)}, f32[5888]{0:T(1024)S(1)}, u32[]{:S(2)}, u32[]{:S(2)}) collective-permute-start(f32[5888]{0:T(1024)S(1)} %concatenate.45), channel_id=1, source_target_pairs={{0,2},{2,0},{1,3},{3,1},{4,6},{6,4},{5,7},{7,5},{8,10},{10,8},{9,1... | collective-permute-start | bytes 70664 | tf_op jit(solution)/shard_map/ppermute | solution.py:20
  485.2 4.7 collective-permute-start.26
  490.6 4.4 collective-permute-start.27
  495.1 6.3 %collective-permute-start.28 = (f32[5888]{0:T(1024)S(1)}, f32[5888]{0:T(1024)S(1)}, u32[]{:S(2)}, u32[]{:S(2)}) collective-permute-start(f32[5888]{0:T(1024)S(1)} %add.162), channel_id=1, source_target_pairs={{0,16},{16,0},{1,17},{17,1},{2,18},{18,2},{3,19},{19,3},{4,20},{20... | collective-permute-start | bytes 70664 | tf_op jit(solution)/shard_map/ppermute | solution.py:20
  (52 other events, 512.4 us)
Sparse Core Ops, SparseCore 0:
  32.7 30.4 all-gather.2
  407.2 22.4 reduce-scatter.7
  431.9 20.4 reduce-scatter.5
  489.3 22.8 reduce-scatter.3
